TPU v7x, 128 devices: a whole 4x4x4 slice. The times are simulated.
128 devices in a mesh: row: 8 (over y_lo, z), col: 2 (over y_hi), tensor: 8 (over x, core).
Axes of the slice: x: 4, y: 4 (y_hi: 2, y_lo: 2; y = y_hi * 2 + y_lo), z: 4, core: 2. Of those that a mesh axis runs over, the one named last changes fastest.
Arguments:
- tokens: bfloat16 [10240, 3072], P(('row', 'col', 'tensor')), may hold values from -6 to 6
- w_query: bfloat16 [3072, 3072], P(None, 'tensor'), may hold values from -0.109375 to 0.109375
- w_key: bfloat16 [3072, 3072], P(None, 'tensor'), may hold values from -0.109375 to 0.109375
- w_value: bfloat16 [3072, 3072], P(None, 'tensor'), may hold values from -0.109375 to 0.109375
- w_out: bfloat16 [3072, 3072], P('tensor'), may hold values from -0.109375 to 0.109375
- w_mod: bfloat16 [512, 18432], P(None, ('row', 'col', 'tensor')), may hold values from -2 to 2
- gain_query: float32 [64], replicated, may hold values from 0.5 to 2.5
- gain_key: float32 [64], replicated, may hold values from 0.5 to 2.5
- timesteps: int32 [2], replicated, may hold values from 0 to 999
- video_lengths: int32 [2], replicated, may hold values from 1 to 6117, 9788 in all
- piece_table: int32 [16], replicated, may hold values from 0 to 15, each once
Outputs:
- update: bfloat16 [10240, 3072], P(('row', 'col', 'tensor'))
Inputs may be any that keep to these rules, and one draw needn't show every extreme that they name: `video_lengths`: the two lengths sum to 9788; the larger one is at most 6117, and which sample has it varies. `piece_table`: each tile index 0 .. 15 appears once.
All inputs are finite; a program needn't handle non-finite values.
Results may differ from a plain program's by a relative error of at most 0.02.
Values may be sent and summed in bfloat16 or wider, within the bound.
No kernel may reach another device: no remote copies, remote signals or barrier semaphores. Data moves between devices by JAX's collectives and lax.ppermute only.
A program may use at most 192 MiB of HBM per device.

v0:
```python
import functools
import math

import jax
import jax.numpy as jnp
from jax import lax
from jax.experimental import pallas as pl
from jax.experimental.pallas import tpu as pltpu
from jax.sharding import Mesh, PartitionSpec as P

HD = 64
TE = 512
TEXT = 226
HP = 30
WP = 45
CAP = 640
D = 3072
BLK = 128
OWN = 80
BIG = 16384.0
F32 = jnp.float32
BF16 = jnp.bfloat16

AXES = ("ylo", "z", "yhi", "x", "core")
Y_AXES = ("ylo", "yhi")
Y_INDEX = (0, 2, 1, 3)
VMEM_LIMIT = 60 * 1024 * 1024
SHIFTS = (1, -1, 2)


def shift_x(value, step):
    return lax.ppermute(value, "x", [(i, (i + step) % 4) for i in range(4)])


def shift_z(value, step):
    return lax.ppermute(value, "z", [(i, (i + step) % 4) for i in range(4)])


def shift_y(value, step):
    return lax.ppermute(value, Y_AXES, [(Y_INDEX[i], Y_INDEX[(i + step) % 4]) for i in range(4)])


def swap_core(value):
    return lax.ppermute(value, "core", [(0, 1), (1, 0)])


def time_features(timesteps):
    half_dim = TE // 2
    freqs = jnp.exp(-math.log(10000.0) * jnp.arange(half_dim, dtype=F32) / half_dim)
    angles = timesteps.astype(F32)[:, None] * freqs[None, :]
    return jnp.concatenate([jnp.cos(angles), jnp.sin(angles)], axis=1)


def rope_tables(piece, boundary):
    token = piece * CAP + lax.broadcasted_iota(jnp.int32, (CAP, 2 * HD), 0)
    lane = lax.broadcasted_iota(jnp.int32, (CAP, 2 * HD), 1)
    inner = token - jnp.where(token >= boundary, boundary, 0)
    is_text = inner < TEXT
    video = jnp.maximum(inner - TEXT, 0)
    frame = video // (HP * WP)
    height = video // WP % HP
    width = video % WP
    pair = lane % HD // 2
    time_pairs = HD // 8
    space_pairs = 3 * HD // 16
    freq_time = 10000.0 ** (-jnp.arange(0, HD // 4, 2, dtype=F32) / (HD // 4))
    freq_space = 10000.0 ** (-jnp.arange(0, 3 * HD // 8, 2, dtype=F32) / (3 * HD // 8))
    freq = jnp.concatenate([freq_time, freq_space, freq_space])
    freq = jnp.tile(jnp.repeat(freq, 2), 2)[None, :]
    place = jnp.where(
        pair < time_pairs, frame, jnp.where(pair < time_pairs + space_pairs, height, width)
    )
    angle = place.astype(F32) * freq
    cosine = jnp.where(is_text, 1.0, jnp.cos(angle))
    sine = jnp.where(is_text, 0.0, jnp.sin(angle))
    return cosine, jnp.where(lane % 2 == 0, -sine, sine)


def project_kernel(
    info, c0, c1, c2, c3, c4, c5, c6, c7, mods, wq_far, wk_far, wv_far, cos, sin, gq, gk,
    along_z, along_y, rows_in, wq, wk, wv, qa, kva, qb, kvb, middle, sems,
):
    chunks = (c0, c1, c2, c3, c4, c5, c6, c7)
    arrivals = [
        pltpu.make_async_copy(
            chunk, rows_in.at[pl.ds(pl.multiple_of(info[i], 16), OWN), :], sems.at[3 + i]
        )
        for i, chunk in enumerate(chunks)
    ]
    copies = [
        pltpu.make_async_copy(source, target, sems.at[i])
        for i, (source, target) in enumerate(((wq_far, wq), (wk_far, wk), (wv_far, wv)))
    ]
    for copy in arrivals + copies:
        copy.start()
    gain_q = jnp.concatenate([gq[...], gq[...]], axis=1)
    gain_k = jnp.concatenate([gk[...], gk[...]], axis=1)
    for copy in arrivals:
        copy.wait()
    piece = info[8]
    boundary = info[9]
    line = lax.broadcasted_iota(jnp.int32, (256, 128), 0)
    average = jnp.where(
        line % 128 // HD == lax.broadcasted_iota(jnp.int32, (256, 128), 1) // HD, 1.0 / HD, 0.0
    ).astype(BF16)
    even = lax.broadcasted_iota(jnp.int32, (BLK, 128), 1) % 2 == 0

    def head_mean(entries):
        high = entries.astype(BF16)
        low = (entries - high.astype(F32)).astype(BF16)
        return jnp.dot(
            jnp.concatenate([high, low], axis=1), average, preferred_element_type=F32
        )

    def head_prepare(entries, gain, block):
        center = entries - head_mean(entries)
        variance = head_mean(center * center)
        normed = center * lax.rsqrt(variance + 1e-06) * gain
        other = jnp.where(even, pltpu.roll(normed, 127, 1), pltpu.roll(normed, 1, 1))
        place = slice(block * BLK, (block + 1) * BLK)
        return normed * cos[place, :] + other * sin[place, :]

    for block in range(CAP // BLK):
        place = slice(block * BLK, (block + 1) * BLK)
        values = rows_in[place, :].astype(F32)
        center = values - jnp.mean(values, axis=1, keepdims=True)
        variance = jnp.mean(center * center, axis=1, keepdims=True)
        normed = center * lax.rsqrt(variance + 1e-05)
        token = piece * CAP + block * BLK + lax.broadcasted_iota(jnp.int32, (BLK, 1), 0)
        second = token >= boundary
        text = token - jnp.where(second, boundary, 0) < TEXT

        def pick(part):
            video_cols = slice(part * D, (part + 1) * D)
            text_cols = slice((part + 3) * D, (part + 4) * D)
            video_pick = jnp.where(second, mods[1:2, video_cols], mods[0:1, video_cols])
            text_pick = jnp.where(second, mods[1:2, text_cols], mods[0:1, text_cols])
            return jnp.where(text, text_pick, video_pick)

        modded = (normed * (1.0 + pick(1)) + pick(0)).astype(BF16)
        if block == 0:
            for copy in copies:
                copy.wait()
        query = jnp.dot(modded, wq[...], preferred_element_type=F32)
        key = jnp.dot(modded, wk[...], preferred_element_type=F32)
        value = jnp.dot(modded, wv[...], preferred_element_type=F32)
        base = block * 192
        for group in range(3):
            cols = slice(group * 128, (group + 1) * 128)
            q_turn = head_prepare(query[:, cols], gain_q, block).T.astype(BF16)
            v_turn = value[:, cols].T.astype(BF16)
            k_rows = head_prepare(key[:, cols], gain_k, block)
            if group == 0:
                qa[base : base + 128, :] = q_turn
                kva[960 + base : 960 + base + 128, :] = v_turn
                kva[place, :] = k_rows.astype(BF16)
            elif group == 1:
                qa[base + 128 : base + 192, :] = q_turn[:64]
                qb[base + 128 : base + 192, :] = q_turn[64:]
                kva[960 + base + 128 : 960 + base + 192, :] = v_turn[:64]
                kvb[960 + base + 128 : 960 + base + 192, :] = v_turn[64:]
                middle[place, :] = k_rows
            else:
                qb[base : base + 128, :] = q_turn
                kvb[960 + base : 960 + base + 128, :] = v_turn
                kvb[place, :] = k_rows.astype(BF16)
    left = lax.broadcasted_iota(jnp.int32, (CAP // 2, 128), 1) < HD
    upper = middle[: CAP // 2, :]
    lower = middle[CAP // 2 :, :]
    kva[CAP:960, :] = jnp.where(left, upper, pltpu.roll(lower, HD, 1)).astype(BF16)
    kvb[CAP:960, :] = jnp.where(left, pltpu.roll(upper, HD, 1), lower).astype(BF16)
    along_z[:960, :] = qa[...]
    along_z[960:, :] = kvb[...]
    along_y[:960, :] = qb[...]
    along_y[960:, :] = kva[...]


def project(info, chunks, mods, wq, wk, wv, cos, sin, gq, gk):
    vmem = pl.BlockSpec(memory_space=pltpu.VMEM)
    return pl.pallas_call(
        project_kernel,
        out_shape=[jax.ShapeDtypeStruct((2880, 128), BF16)] * 2,
        in_specs=[pl.BlockSpec(memory_space=pltpu.SMEM)]
        + [pl.BlockSpec(memory_space=pl.ANY)] * 8
        + [vmem]
        + [pl.BlockSpec(memory_space=pl.ANY)] * 3
        + [vmem] * 4,
        out_specs=[vmem] * 2,
        scratch_shapes=[pltpu.VMEM((CAP, D), BF16)]
        + [pltpu.VMEM((D, 384), BF16)] * 3
        + [pltpu.VMEM((960, 128), BF16), pltpu.VMEM((1920, 128), BF16)] * 2
        + [pltpu.VMEM((CAP, 128), F32), pltpu.SemaphoreType.DMA((11,))],
        compiler_params=pltpu.CompilerParams(vmem_limit_bytes=VMEM_LIMIT),
        name="project",
    )(info, *chunks, mods, wq, wk, wv, cos, sin, gq, gk)


def attend_kernel(limits, *refs, places, n_k, carried, last):
    n_q = len(places)
    queries, refs = refs[:n_q], refs[n_q:]
    keys, refs = refs[:n_k], refs[n_k:]
    if carried:
        before, refs = refs[0], refs[1:]
    n_out = n_q if last else 1
    outs, refs = refs[:n_out], refs[n_out:]
    qs, ks, vs, todo = refs[:4]
    acc = refs[4] if last else outs[0]
    scale = math.log2(math.e) / math.sqrt(HD)
    half = CAP // 2
    ones = jnp.where(lax.broadcasted_iota(jnp.int32, (16, CAP), 0) == 0, 1.0, 0.0).astype(BF16)
    blank = jnp.zeros((HD, CAP), BF16)

    kinds = [
        jnp.where(limits[4 + tile] == CAP, 0, jnp.where(limits[4 + tile] == 0, 2, 1))
        for tile in range(n_k)
    ]
    slots = []
    only_first = jnp.int32(0)
    only_second = jnp.int32(0)
    key_limit = jnp.int32(0)
    for tile in range(n_k):
        slot = jnp.int32(0)
        for other in range(n_k):
            if other < tile:
                slot = slot + jnp.where(kinds[other] <= kinds[tile], 1, 0)
            elif other > tile:
                slot = slot + jnp.where(kinds[other] < kinds[tile], 1, 0)
        slots.append(slot)
        only_first = only_first + jnp.where(kinds[tile] == 0, 1, 0)
        only_second = only_second + jnp.where(kinds[tile] == 2, 1, 0)
        key_limit = key_limit + limits[4 + tile]
    for i, place in enumerate(places):
        has_first = limits[place] > 0
        has_second = limits[place] < CAP
        todo[16 + i] = limits[place]
        if carried and place != 3:
            shared = (has_first & (limits[7] > 0)) | (has_second & (limits[7] < CAP))
            todo[i] = slots[3]
            todo[8 + i] = jnp.where(shared, 1, 0)
        else:
            low = jnp.where(has_first, 0, only_first)
            todo[i] = low
            todo[8 + i] = jnp.where(has_second, n_k, n_k - only_second) - low

    for tile in range(n_k):
        start = pl.multiple_of(slots[tile] * CAP, 64)
        ks[0, pl.ds(start, CAP), :] = keys[tile][:CAP, :]
        end = keys[tile][CAP:960, :]
        ks[1, pl.ds(start, half), :] = end
        ks[1, pl.ds(start + half, half), :] = jnp.concatenate([end[:, HD:], end[:, :HD]], axis=1)
        vs[pl.ds(pl.multiple_of(slots[tile] * 960, 64), 960), :] = keys[tile][960:, :]
    for i, place in enumerate(places):
        for head in range(3):
            at = HD if head == 1 else 0
            qs[i, head, HD - at : 2 * HD - at, :] = blank
            for block in range(5):
                row = 192 * block + HD * head
                cols = slice(128 * block, 128 * block + 128)
                qs[i, head, at : at + HD, cols] = queries[i][row : row + HD, :]
        if carried and place != 3:
            acc[i] = before[i]
        else:
            acc[i] = jnp.zeros((3, 80, CAP), F32)

    def part(i, head, slot, count, masked):
        first = pl.multiple_of(slot * CAP, 64)
        bank = jnp.where(head == 2, 1, 0)
        scores = jnp.dot(
            ks[bank, pl.ds(first, count * CAP), :], qs[i, head], preferred_element_type=F32
        )
        weights = jnp.exp2(scores * scale).astype(BF16)
        columns = []
        for block in range(5 * count):
            start = slot * 960 + head * HD + 192 * block
            columns.append(vs[pl.ds(pl.multiple_of(start, HD), HD), :])
        value = jnp.concatenate(
            [jnp.concatenate(columns, axis=1), jnp.concatenate([ones] * count, axis=1)], axis=0
        )
        place = first + lax.broadcasted_iota(jnp.int32, value.shape, 1)
        k_second = jnp.where(place >= key_limit, 1, 0)
        nothing = jnp.zeros_like(value)
        if masked:
            value = jnp.concatenate(
                [
                    jnp.where(k_second == 0, value, nothing),
                    jnp.where(k_second == 1, value, nothing),
                ],
                axis=0,
            )
            both = jnp.dot(value, weights, preferred_element_type=F32)
            q_second = lax.broadcasted_iota(jnp.int32, (80, CAP), 1) >= todo[16 + i]
            acc[i, head] += jnp.where(q_second, both[80:], both[:80])
        else:
            sample = jnp.where(todo[16 + i] > 0, 0, 1)
            value = jnp.where(k_second == sample, value, nothing)
            acc[i, head] += jnp.dot(value, weights, preferred_element_type=F32)

    def heads(i, slot, count, masked):
        def one_head(head, rest):
            part(i, head, slot, count, masked)
            return rest

        lax.fori_loop(0, 3, one_head, 0)

    def q_tile(i, carry):
        low = todo[i]
        count = todo[8 + i]
        limit = todo[16 + i]
        mixed = (limit > 0) & (limit < CAP)

        @pl.when(mixed)
        def _():
            def one(step, inner):
                heads(i, low + step, 1, True)
                return inner

            lax.fori_loop(0, count, one, 0)

        @pl.when(jnp.logical_not(mixed))
        def _():
            def two(step, inner):
                heads(i, low + 2 * step, 2, False)
                return inner

            lax.fori_loop(0, count // 2, two, 0)

            @pl.when(count % 2 == 1)
            def _():
                heads(i, low + count - 1, 1, False)

        return carry

    lax.fori_loop(0, n_q, q_tile, 0)
    if last:
        for i, (place, ref) in enumerate(zip(places, outs)):
            if place == 0:
                ref[...] = acc[i]
                continue
            sums = jnp.concatenate([acc[i, head, HD : HD + 1, :] for head in range(3)], axis=0)
            high = sums.astype(BF16)
            low = (sums - high.astype(F32)).astype(BF16)
            for head in range(3):
                ref[HD * head : HD * head + HD, :] = acc[i, head, :HD, :].astype(BF16)
            ref[192:195, :] = high
            ref[195:198, :] = low
            ref[198:208, :] = jnp.zeros((10, CAP), BF16)


def attend(limits, queries, keys, places, name, before=None):
    vmem = pl.BlockSpec(memory_space=pltpu.VMEM)
    n_q, n_k = len(places), len(keys)
    carried = before is not None
    last = n_k == 4
    if last:
        out_shape = [
            jax.ShapeDtypeStruct((208, CAP), BF16)
            if place
            else jax.ShapeDtypeStruct((3, 80, CAP), F32)
            for place in places
        ]
    else:
        out_shape = [jax.ShapeDtypeStruct((n_q, 3, 80, CAP), F32)]
    scratch = [
        pltpu.VMEM((n_q, 3, 128, CAP), BF16),
        pltpu.VMEM((2, n_k * CAP, 128), BF16),
        pltpu.VMEM((n_k * 960, 128), BF16),
        pltpu.SMEM((24,), jnp.int32),
    ]
    if last:
        scratch.append(pltpu.VMEM((n_q, 3, 80, CAP), F32))
    q_spec = pl.BlockSpec((960, 128), lambda i: (0, 0))
    k_spec = pl.BlockSpec((pl.Element(1920), pl.Element(128)), lambda i: (960, 0))
    operands = [limits, *queries, *keys] + ([before] if carried else [])
    specs = [pl.BlockSpec(memory_space=pltpu.SMEM)] + [q_spec] * n_q + [k_spec] * n_k
    return pl.pallas_call(
        functools.partial(attend_kernel, places=places, n_k=n_k, carried=carried, last=last),
        out_shape=out_shape,
        grid=(1,),
        in_specs=specs + [vmem] * (len(operands) - len(specs)),
        out_specs=[vmem] * len(out_shape),
        scratch_shapes=scratch,
        cost_estimate=pl.CostEstimate(flops=1000, transcendentals=0, bytes_accessed=1000),
        compiler_params=pltpu.CompilerParams(vmem_limit_bytes=VMEM_LIMIT),
        name=name,
    )(*operands)


def merge_kernel(
    order, own_a, a1, a2, a3, own_b, b1, b2, b3, theirs, mine, turned, rows
):
    for own, others, heads in (
        (own_a, (a1, a2, a3), (0, 1, 2)),
        (own_b, (b1, b2, b3), (4, 5, 3)),
    ):
        for place, head in enumerate(heads):
            total = own[place, :HD, :]
            share = own[place, HD : HD + 1, :]
            for ref in others:
                total = total + ref[HD * place : HD * place + HD, :].astype(F32)
                tail = ref[192:208, :].astype(F32)
                share = share + tail[place : place + 1, :] + tail[3 + place : 4 + place, :]
            turned[HD * head : HD * head + HD, :] = total / share

    def turn(block, carry):
        place = pl.ds(pl.multiple_of(block * 128, 128), 128)
        for group in range(3):
            cols = slice(group * 128, group * 128 + 128)
            rows[place, cols] = turned[cols, place].T.astype(BF16)
        return carry

    lax.fori_loop(0, 5, turn, 0)
    for i in range(4):
        start = pl.multiple_of(order[i], 16)
        theirs[i * OWN : (i + 1) * OWN, :] = rows[pl.ds(start, OWN), :]
        start = pl.multiple_of(order[4 + i], 16)
        mine[i * OWN : (i + 1) * OWN, :] = rows[pl.ds(start, OWN), :]


def merge(order, own_a, others_a, own_b, others_b):
    vmem = pl.BlockSpec(memory_space=pltpu.VMEM)
    return pl.pallas_call(
        merge_kernel,
        out_shape=[jax.ShapeDtypeStruct((4 * OWN, 384), BF16)] * 2,
        in_specs=[pl.BlockSpec(memory_space=pltpu.SMEM)] + [vmem] * 8,
        out_specs=[vmem] * 2,
        scratch_shapes=[pltpu.VMEM((384, CAP), F32), pltpu.VMEM((CAP, 384), BF16)],
        compiler_params=pltpu.CompilerParams(vmem_limit_bytes=VMEM_LIMIT),
        name="merge",
    )(order, own_a, *others_a, own_b, *others_b)


def far_output_kernel(mine, theirs, w_here, w_other, out):
    rows = slice(3 * OWN, 4 * OWN)

    def step(i, carry):
        cols = pl.ds(pl.multiple_of(i * 768, 128), 768)
        total = jnp.dot(mine[rows, :], w_here[:, cols], preferred_element_type=F32)
        total += jnp.dot(theirs[rows, :], w_other[:, cols], preferred_element_type=F32)
        out[:, cols] = total.astype(BF16)
        return carry

    lax.fori_loop(0, D // 768, step, 0)


def far_output(mine, theirs, w_here, w_other):
    vmem = pl.BlockSpec(memory_space=pltpu.VMEM)
    return pl.pallas_call(
        far_output_kernel,
        out_shape=jax.ShapeDtypeStruct((OWN, D), BF16),
        in_specs=[vmem] * 4,
        out_specs=vmem,
        cost_estimate=pl.CostEstimate(flops=1000, transcendentals=0, bytes_accessed=1000),
        compiler_params=pltpu.CompilerParams(vmem_limit_bytes=VMEM_LIMIT),
        name="far_output",
    )(mine, theirs, w_here, w_other)


def near_output_kernel(mine, theirs, r1, r2, *refs):
    far, out, held, left, sems = refs[:6], refs[6], refs[7], refs[8], refs[9]
    for i, source in enumerate(far):
        pltpu.make_async_copy(source, held.at[i], sems.at[i]).start()
    rows = (mine[:OWN, :], theirs[:OWN, :], r1[:OWN, :], r1[OWN:, :], r2[:OWN, :], r2[OWN:, :])
    for i, entries in enumerate(rows):
        left[i] = entries
    out[...] = jnp.zeros_like(out)

    def step(i, carry):
        pltpu.make_async_copy(far[0], held.at[i], sems.at[i]).wait()
        out[...] += jnp.dot(left[i], held[i], preferred_element_type=F32)
        return carry

    lax.fori_loop(0, 6, step, 0)


def near_output(mine, theirs, r1, r2, weights):
    vmem = pl.BlockSpec(memory_space=pltpu.VMEM)
    return pl.pallas_call(
        near_output_kernel,
        out_shape=jax.ShapeDtypeStruct((OWN, D), F32),
        in_specs=[vmem] * 4 + [pl.BlockSpec(memory_space=pl.ANY)] * 6,
        out_specs=vmem,
        scratch_shapes=[
            pltpu.VMEM((6, 384, D), BF16),
            pltpu.VMEM((6, OWN, 384), BF16),
            pltpu.SemaphoreType.DMA((6,)),
        ],
        compiler_params=pltpu.CompilerParams(vmem_limit_bytes=VMEM_LIMIT),
        name="near_output",
    )(mine, theirs, r1, r2, *weights)


def select_gate(modulation, second, text):
    video_cols = modulation[:, 2 * D : 3 * D]
    text_cols = modulation[:, 5 * D : 6 * D]
    video_pick = jnp.where(second, video_cols[1][None, :], video_cols[0][None, :])
    text_pick = jnp.where(second, text_cols[1][None, :], text_cols[0][None, :])
    return jnp.where(text, text_pick, video_pick)


def local(
    tokens, w_query, w_key, w_value, w_out, w_mod, gain_query, gain_key, timesteps,
    video_lengths, piece_table,
):
    x, core = lax.axis_index("x"), lax.axis_index("core")
    z = lax.axis_index("z")
    y = lax.axis_index("yhi") * 2 + lax.axis_index("ylo")
    boundary = TEXT + video_lengths[0]

    across = [tokens] + [shift_x(tokens, step) for step in SHIFTS]
    chunks = across + [swap_core(chunk) for chunk in across]

    w_other = swap_core(w_out)

    act = jax.nn.silu(time_features(timesteps)).astype(BF16)
    part_mod = jnp.dot(act, w_mod, preferred_element_type=F32)
    width = part_mod.shape[1]
    packed = jnp.pad(part_mod.reshape(2 * width), (0, 384 - 2 * width)).reshape(3, 128)
    tiles_axes = ("ylo", "z", "yhi")
    spread = lax.all_to_all(
        jnp.broadcast_to(packed[None], (16, 3, 128)), tiles_axes, 0, 0, tiled=True
    )
    spread = lax.all_to_all(
        jnp.broadcast_to(spread[None], (8, 16, 3, 128)), ("x", "core"), 0, 0, tiled=True
    )
    spread = spread.transpose(1, 0, 2, 3).reshape(128, 384)
    modulation = jnp.stack(
        [spread[:, :width].reshape(128 * width), spread[:, width : 2 * width].reshape(128 * width)]
    )

    back = jnp.array([0, 1, -1, 2], jnp.int32)
    z_ring = (z - back) % 4
    y_ring = (y - back) % 4
    z_tiles = ((y % 2) * 4 + z_ring) * 2 + y // 2
    y_tiles = ((y_ring % 2) * 4 + z) * 2 + y_ring // 2
    tiles = jnp.concatenate([z_tiles, y_tiles])
    pieces = jnp.sum(
        jnp.where(
            tiles[:, None] == jnp.arange(16, dtype=jnp.int32)[None, :], piece_table[None, :], 0
        ),
        axis=1,
    )
    limits_a = jnp.clip(boundary - pieces * CAP, 0, CAP)
    limits_b = jnp.concatenate([limits_a[4:], limits_a[:4]])
    piece = pieces[0]
    x_ring = (x - back) % 4
    starts = jnp.concatenate([(x_ring * 2 + core) * OWN, (x_ring * 2 + 1 - core) * OWN])
    info = jnp.concatenate([starts, jnp.stack([piece, boundary])])

    cos, sin = rope_tables(piece, boundary)
    along_z, along_y = project(
        info, chunks, modulation, w_query, w_key, w_value, cos, sin, gain_query[None, :],
        gain_key[None, :],
    )
    from_z = [along_z] + [shift_z(along_z, step) for step in SHIFTS]
    from_y = [along_y] + [shift_y(along_y, step) for step in SHIFTS]
    limits_a, w_other, w_late, _ = lax.optimization_barrier(
        (limits_a, w_other, w_out, (from_z[1:3], from_y[1:3]))
    )
    w_behind, w_ahead = shift_x(w_late, 1), shift_x(w_late, -1)
    v_behind, v_ahead = swap_core(w_behind), swap_core(w_ahead)
    near_a = attend(limits_a, from_z[:3], from_y[:3], (0, 1, 2), "near_a")[0]
    own_a, *parts_a = attend(limits_a, from_z, from_y, (0, 1, 2, 3), "far_a", near_a)
    sent_a = [shift_z(part, -step) for part, step in zip(parts_a, SHIFTS)]
    limits_b, _ = lax.optimization_barrier((limits_b, parts_a[0]))
    parts_b = attend(limits_b, from_y[1:], from_z, (1, 2, 3), "rest_b")
    sent_b = [shift_y(part, -step) for part, step in zip(parts_b, SHIFTS)]
    limits_b, _ = lax.optimization_barrier((limits_b, (parts_b[0], sent_a)))
    own_b = attend(limits_b, from_y[:1], from_z, (0,), "own_b")[0]

    ahead = (x + back) % 4
    order = jnp.concatenate([(ahead * 2 + 1 - core) * OWN, (ahead * 2 + core) * OWN])
    theirs, mine = merge(order, own_a, sent_a, own_b, sent_b)
    received = swap_core(theirs)
    share = shift_x(far_output(mine, received, w_out, w_other), 2)
    arrived = []
    for i, step in ((1, 1), (2, -1)):
        rows = slice(i * OWN, (i + 1) * OWN)
        arrived.append(shift_x(jnp.concatenate([mine[rows], received[rows]]), step))
    projection = near_output(
        mine, received, *arrived, (w_out, w_other, w_behind, v_behind, w_ahead, v_ahead)
    )
    projection = projection + share.astype(F32)

    own_token = piece * CAP + starts[0] + jnp.arange(OWN, dtype=jnp.int32)[:, None]
    second = own_token >= boundary
    text = own_token - jnp.where(second, boundary, 0) < TEXT
    gate = select_gate(modulation, second, text)
    return (gate * projection).astype(BF16)


def solution(mesh):
    fine = Mesh(mesh.devices.reshape(2, 4, 2, 4, 2), AXES)
    tensor = ("x", "core")
    placed = (
        P(AXES, None),
        P(None, tensor),
        P(None, tensor),
        P(None, tensor),
        P(tensor, None),
        P(None, AXES),
        P(),
        P(),
        P(),
        P(),
        P(),
    )
    return jax.shard_map(
        local, mesh=fine, in_specs=placed, out_specs=P(AXES, None), check_vma=False
    )
```

profile of v0, /device:TPU:0, one launch (start us, length us, event | category | flops | bytes accessed | tf_op | source)
XLA Modules:
  0.0 176.3 jit_solution(16329542548117629296)
XLA Ops:
  0.0 1.6 collective-permute-start.1
  1.6 1.7 collective-permute-start.2
  3.2 1.9 %collective-permute-start.3 = (bf16[80,3072]{1,0:T(8,128)(2,1)}, bf16[80,3072]{1,0:T(8,128)(2,1)S(1)}, u32[]{:S(2)}, u32[]{:S(2)}) collective-permute-start(bf16[80,3072]{1,0:T(8,128)(2,1)} %c0.1), channel_id=1, source_target_pairs={{0,4},{2,6},{4,0},{6,2},{1,5},{3,7},{5,1},{7,3},{8,12},{10,14},{12... | collective-permute-start | bytes 1474568 | tf_op jit(solution)/shard_map/ppermute | solution.py:32
  5.1 0.5 collective-permute-start
  5.7 0.7 convert_element_type.17
  6.3 0.1 multiply_cosine_fusion
  6.5 0.1 fusion.19
  6.7 0.6 broadcast_in_dim.120
  7.3 8.0 %all-to-all-start = ((f32[16,3,128]{2,1,0:T(4,128)}), f32[16,3,128]{2,1,0:T(4,128)S(1)}, u32[]{:S(2)}, u32[]{:S(2)}) async-start(f32[16,3,128]{2,1,0:T(4,128)} %broadcast_in_dim.120), calls=%async_computation | async-start | bytes 65536 | tf_op jit(solution)/shard_map/all_to_all | solution.py:519
  15.5 1.2 subtract_multiply_fusion.1
  16.8 0.8 select_reduce_fusion
  18.9 3.0 %negate_select_fusion = (f32[640,128]{1,0:T(8,128)}, f32[640,128]{1,0:T(8,128)}) fusion(s32[128]{0:T(128)S(1)} %get-tuple-element.65, s32[128]{0:T(128)S(1)} %get-tuple-element.67, pred[640]{0:T(1024)(128)(4,1)S(1)} %fusion.13, pred[128]{0:T(512)(128)(4,1)S(1)} %get-tuple-element.63, f32[128]{0:T(128)S(1)} %mul.106, s32[640]{0:T(1024)S(1)} %fusion.15, ...), kind=kLoop, calls=%fused_computation.5 | loop fusion | flops 3031040 | bytes 676096 | tf_op jit(solution)/shard_map/jit(_where)/select_n | solution.py:76
  21.8 1.3 all-to-all-done
  23.1 0.7 broadcast_in_dim.121
  23.8 3.4 %all-to-all-start.1 = ((f32[8,16,3,128]{3,1,2,0:T(8,128)}), f32[8,16,3,128]{3,1,2,0:T(8,128)S(1)}, u32[]{:S(2)}, u32[]{:S(2)}) async-start(f32[8,16,3,128]{3,1,2,0:T(8,128)} %broadcast_in_dim.121), calls=%async_computation.1 | async-start | bytes 393216 | tf_op jit(solution)/shard_map/all_to_all | solution.py:522
  27.2 0.7 pad_add_fusion.2.info
  27.9 6.1 %all-to-all-done.1 = f32[8,16,3,128]{3,1,2,0:T(8,128)S(1)} async-done(((f32[8,16,3,128]{3,1,2,0:T(8,128)}), f32[8,16,3,128]{3,1,2,0:T(8,128)S(1)}, u32[]{:S(2)}, u32[]{:S(2)}) %all-to-all-start.1) | async-done | bytes 196640 | tf_op jit(solution)/shard_map/all_to_all | solution.py:522
  34.1 0.2 stack_reshape.6
  34.3 0.2 stack_reshape.7
  34.6 0.5 collective-permute-start.6
  35.1 0.3 collective-permute-start.7
  35.4 0.8 pad_maximum_fusion.mods
  36.2 0.3 collective-permute-done.5.c5
  36.5 0.7 collective-permute-done.6.c6
  37.2 0.7 collective-permute-done.7.c7
  37.9 0.1 copy-done.13
  38.0 0.7 copy-done.14
  38.7 17.8 %project.1 = (bf16[2880,128]{1,0:T(8,128)(2,1)}, bf16[2880,128]{1,0:T(8,128)(2,1)}) custom-call(s32[10]{0:T(128)} %pad_add_fusion.2.info, bf16[80,3072]{1,0:T(8,128)(2,1)} %c0.1, bf16[80,3072]{1,0:T(8,128)(2,1)} %copy-done.8, bf16[80,3072]{1,0:T(8,128)(2,1)} %copy-done.9, bf16[80,3072]{1,0:T(8,128)(2,1)} %copy-done.10, bf16[80,3072]{1,0:T(8,128)(2,1)} %copy-done.11, ...), custom_call_target="tpu_custom_call" | custom-call | tf_op jit(solution)/shard_map/project/pallas_call | solution.py:180
  56.4 0.7 collective-permute-start.8
  57.1 2.6 %collective-permute-start.9 = (bf16[2880,128]{1,0:T(8,128)(2,1)}, bf16[2880,128]{1,0:T(8,128)(2,1)S(1)}, u32[]{:S(2)}, u32[]{:S(2)}) collective-permute-start(bf16[2880,128]{1,0:T(8,128)(2,1)} %get-tuple-element.21.refs_0_.refs_3_.refs_1_), channel_id=1, source_target_pairs={{0,48},{16,0},{32,16},{48,32},{1,49},{17,1},{33,17},{49,33},{2,50}... | collective-permute-start | bytes 2211848 | tf_op jit(solution)/shard_map/ppermute | solution.py:36
  59.7 0.7 collective-permute-start.10
  60.4 2.6 %collective-permute-start.11 = (bf16[2880,128]{1,0:T(8,128)(2,1)}, bf16[2880,128]{1,0:T(8,128)(2,1)S(1)}, u32[]{:S(2)}, u32[]{:S(2)}) collective-permute-start(bf16[2880,128]{1,0:T(8,128)(2,1)} %get-tuple-element.22.refs_3_.refs_4_.refs_0_), channel_id=1, source_target_pairs={{0,72},{64,0},{8,64},{72,8},{1,73},{65,1},{9,65},{73,9},{2,74},{66... | collective-permute-start | bytes 2211848 | tf_op jit(solution)/shard_map/ppermute | solution.py:40
  63.0 0.7 subtract_clamp_fusion.limits
  63.6 12.8 %collective-permute-done.8.refs_1_.refs_4_.refs_2_ = bf16[2880,128]{1,0:T(8,128)(2,1)S(1)} collective-permute-done((bf16[2880,128]{1,0:T(8,128)(2,1)}, bf16[2880,128]{1,0:T(8,128)(2,1)S(1)}, u32[]{:S(2)}, u32[]{:S(2)}) %collective-permute-start.8) | collective-permute-done | bytes 737312 | tf_op jit(solution)/shard_map/ppermute | solution.py:36
  76.4 2.7 %collective-permute-done.10.refs_4_.refs_5_.refs_0_ = bf16[2880,128]{1,0:T(8,128)(2,1)S(1)} collective-permute-done((bf16[2880,128]{1,0:T(8,128)(2,1)}, bf16[2880,128]{1,0:T(8,128)(2,1)S(1)}, u32[]{:S(2)}, u32[]{:S(2)}) %collective-permute-start.10) | collective-permute-done | bytes 737312 | tf_op jit(solution)/shard_map/ppermute | solution.py:40
  79.1 0.6 collective-permute-start.23
  79.8 2.7 %collective-permute-start.25 = (bf16[384,3072]{1,0:T(8,128)(2,1)S(1)}, bf16[384,3072]{1,0:T(8,128)(2,1)}, u32[]{:S(2)}, u32[]{:S(2)}) collective-permute-start(bf16[384,3072]{1,0:T(8,128)(2,1)S(1)} %copy-done.3), channel_id=1, source_target_pairs={{0,6},{2,0},{4,2},{6,4},{1,7},{3,1},{5,3},{7,5},{8,14},{10,8},{12,... | collective-permute-start | bytes 7077896 | tf_op jit(solution)/shard_map/ppermute | solution.py:32
  82.5 0.9 collective-permute-start.12
  83.4 2.6 %collective-permute-start.13 = (bf16[2880,128]{1,0:T(8,128)(2,1)}, bf16[2880,128]{1,0:T(8,128)(2,1)}, u32[]{:S(2)}, u32[]{:S(2)}) collective-permute-start(bf16[2880,128]{1,0:T(8,128)(2,1)} %get-tuple-element.22.refs_3_.refs_4_.refs_0_), channel_id=1, source_target_pairs={{0,8},{64,72},{8,0},{72,64},{1,9},{65,73},{9,1},{73,65},{2,10},{66... | collective-permute-start | bytes 2211848 | tf_op jit(solution)/shard_map/ppermute | solution.py:40
  86.0 0.6 fusion.46
  86.7 12.8 %near_a.1.refs_8_ = f32[3,3,80,640]{3,2,1,0:T(8,128)} custom-call(s32[8]{0:T(128)} %copy-done.20, bf16[2880,128]{1,0:T(8,128)(2,1)} %get-tuple-element.21.refs_0_.refs_3_.refs_1_, bf16[2880,128]{1,0:T(8,128)(2,1)} %copy-done.1, bf16[2880,128]{1,0:T(8,128)(2,1)} %copy-done.2, bf16[2880,128]{1,0:T(8,128)(2,1)} %get-tuple-element.22.refs_3_.refs_4_.refs_0_, ...), custom_call_target="tpu_custom_call" | custom-call | flops 1000 | bytes 1000 | tf_op jit(solution)/shard_map/near_a/pallas_call | solution.py:375
  99.5 1.2 collective-permute-done.12.refs_3_.refs_6_.refs_4_
  100.8 0.7 collective-permute-done.13.refs_7_.refs_2_
  101.4 10.2 %far_a.1 = (f32[3,80,640]{2,1,0:T(8,128)}, bf16[208,640]{1,0:T(8,128)(2,1)}, bf16[208,640]{1,0:T(8,128)(2,1)}, bf16[208,640]{1,0:T(8,128)(2,1)}) custom-call(s32[8]{0:T(128)} %copy-done.20, bf16[2880,128]{1,0:T(8,128)(2,1)} %get-tuple-element.21.refs_0_.refs_3_.refs_1_, bf16[2880,128]{1,0:T(8,128)(2,1)} %copy-done.1, bf16[2880,128]{1,0:T(8,128)(2,1)} %copy-done.2, ...), custom_call_target="tpu_custom_call" | custom-call | flops 1000 | bytes 1000 | tf_op jit(solution)/shard_map/far_a/pallas_call | solution.py:375
  111.7 5.7 %collective-permute-start.14 = (bf16[208,640]{1,0:T(8,128)(2,1)}, bf16[208,640]{1,0:T(8,128)(2,1)S(1)}, u32[]{:S(2)}, u32[]{:S(2)}) collective-permute-start(bf16[208,640]{1,0:T(8,128)(2,1)} %get-tuple-element.25), channel_id=1, source_target_pairs={{0,48},{16,0},{32,16},{48,32},{1,49},{17,1},{33,17},{49,33},{2,50}... | collective-permute-start | bytes 798728 | tf_op jit(solution)/shard_map/ppermute | solution.py:36
  117.4 1.5 collective-permute-start.16
  118.9 0.7 pad_add_fusion.3.limits
  119.6 0.5 add_multiply_fusion
  120.1 13.9 %rest_b.1 = (bf16[208,640]{1,0:T(8,128)(2,1)}, bf16[208,640]{1,0:T(8,128)(2,1)}, bf16[208,640]{1,0:T(8,128)(2,1)}) custom-call(s32[8]{0:T(128)} %pad_add_fusion.3.limits, bf16[2880,128]{1,0:T(8,128)(2,1)} %copy-done.4, bf16[2880,128]{1,0:T(8,128)(2,1)} %copy-done.5, bf16[2880,128]{1,0:T(8,128)(2,1)} %collective-permute-done.13.refs_7_.refs_2_, ...), custom_call_target="tpu_custom_call" | custom-call | flops 1000 | bytes 1000 | tf_op jit(solution)/shard_map/rest_b/pallas_call | solution.py:375
  134.1 2.0 %collective-permute-start.18 = (bf16[208,640]{1,0:T(8,128)(2,1)}, bf16[208,640]{1,0:T(8,128)(2,1)}, u32[]{:S(2)}, u32[]{:S(2)}) collective-permute-start(bf16[208,640]{1,0:T(8,128)(2,1)} %get-tuple-element.31), channel_id=1, source_target_pairs={{0,64},{64,8},{8,72},{72,0},{1,65},{65,9},{9,73},{73,1},{2,66},{66... | collective-permute-start | bytes 798728 | tf_op jit(solution)/shard_map/ppermute | solution.py:40
  136.2 0.6 copy-done.17
  136.8 1.2 pad_add_fusion.1.order
  138.0 5.1 %own_b.1 = f32[3,80,640]{2,1,0:T(8,128)} custom-call(s32[8]{0:T(128)} %pad_add_fusion.3.limits, bf16[2880,128]{1,0:T(8,128)(2,1)} %get-tuple-element.22.refs_3_.refs_4_.refs_0_, bf16[2880,128]{1,0:T(8,128)(2,1)} %get-tuple-element.21.refs_0_.refs_3_.refs_1_, bf16[2880,128]{1,0:T(8,128)(2,1)} %copy-done.1, bf16[2880,128]{1,0:T(8,128)(2,1)} %copy-done.2, ...), custom_call_target="tpu_custom_call" | custom-call | flops 1000 | bytes 1000 | tf_op jit(solution)/shard_map/own_b/pallas_call | solution.py:375
  143.2 3.1 %collective-permute-done.18.b2 = bf16[208,640]{1,0:T(8,128)(2,1)} collective-permute-done((bf16[208,640]{1,0:T(8,128)(2,1)}, bf16[208,640]{1,0:T(8,128)(2,1)}, u32[]{:S(2)}, u32[]{:S(2)}) %collective-permute-start.18) | collective-permute-done | bytes 266272 | tf_op jit(solution)/shard_map/ppermute | solution.py:40
  146.3 3.4 %merge.1 = (bf16[320,384]{1,0:T(8,128)(2,1)}, bf16[320,384]{1,0:T(8,128)(2,1)}) custom-call(s32[8]{0:T(128)} %pad_add_fusion.1.order, f32[3,80,640]{2,1,0:T(8,128)} %get-tuple-element.24.own_a, bf16[208,640]{1,0:T(8,128)(2,1)} %copy-done.15, bf16[208,640]{1,0:T(8,128)(2,1)} %copy-done.16, bf16[208,640]{1,0:T(8,128)(2,1)} %copy-done.17, f32[3,80,640]{2,1,0:T(8,128)} %own_b.1, ...), custom_call_target="tpu_custom_call" | custom-call | tf_op jit(solution)/shard_map/merge/pallas_call | solution.py:421
  149.7 0.9 fusion.41
  150.6 0.8 collective-permute-done.20.theirs
  151.6 3.3 %collective-permute-start.22 = (bf16[160,384]{1,0:T(8,128)(2,1)S(1)}, bf16[160,384]{1,0:T(8,128)(2,1)S(1)}, u32[]{:S(2)}, u32[]{:S(2)}) collective-permute-start(bf16[160,384]{1,0:T(8,128)(2,1)S(1)} %pad_maximum_fusion.2), channel_id=1, source_target_pairs={{0,6},{2,0},{4,2},{6,4},{1,7},{3,1},{5,3},{7,5},{8,14},{10,8},{12,... | collective-permute-start | bytes 368648 | tf_op jit(solution)/shard_map/ppermute | solution.py:32
  154.8 4.8 %far_output.1 = bf16[80,3072]{1,0:T(8,128)(2,1)} custom-call(bf16[320,384]{1,0:T(8,128)(2,1)} %get-tuple-element.33.mine, bf16[320,384]{1,0:T(8,128)(2,1)} %copy-done.7, bf16[384,3072]{1,0:T(8,128)(2,1)} %w_here.1, bf16[384,3072]{1,0:T(8,128)(2,1)} %collective-permute-done.refs_1_.w_other), custom_call_target="tpu_custom_call" | custom-call | flops 1000 | bytes 1000 | tf_op jit(solution)/shard_map/far_output/pallas_call | solution.py:447
  159.7 0.6 copy-done.18
  160.4 1.4 copy-done.6
  161.8 7.9 %near_output.1 = f32[80,3072]{1,0:T(8,128)} custom-call(bf16[320,384]{1,0:T(8,128)(2,1)} %get-tuple-element.33.mine, bf16[320,384]{1,0:T(8,128)(2,1)} %copy-done.7, bf16[160,384]{1,0:T(8,128)(2,1)} %copy-done.18, bf16[160,384]{1,0:T(8,128)(2,1)} %copy-done.19, bf16[384,3072]{1,0:T(8,128)(2,1)} %w_here.1, ...), custom_call_target="tpu_custom_call" | custom-call | tf_op jit(solution)/shard_map/near_output/pallas_call | solution.py:477
  169.7 4.3 %collective-permute-done.27 = bf16[80,3072]{1,0:T(8,128)(2,1)S(1)} collective-permute-done((bf16[80,3072]{1,0:T(8,128)(2,1)}, bf16[80,3072]{1,0:T(8,128)(2,1)S(1)}, u32[]{:S(2)}, u32[]{:S(2)}) %collective-permute-start.27) | collective-permute-done | bytes 491552 | tf_op jit(solution)/shard_map/ppermute | solution.py:32
  174.1 2.3 %multiply_convert_fusion = bf16[80,3072]{1,0:T(8,128)(2,1)} fusion(f32[80,3072]{1,0:T(8,128)} %near_output.1, bf16[80,3072]{1,0:T(8,128)(2,1)S(1)} %collective-permute-done.27, f32[3072]{0:T(1024)S(1)} %bitcast.22, f32[3072]{0:T(1024)S(1)} %bitcast.24, f32[3072]{0:T(1024)S(1)} %bitcast.21, f32[3072]{0:T(1024)S(1)} %bitcast.23, pred[80]{0:T(512)(128)(4,1)S(1)} %fusion.36, ...), kind=kLoop, calls=%fused_computation | loop fusion | flops 1720320 | bytes 2015392 | tf_op jit(solution)/shard_map/convert_element_type | solution.py:588
  (112 shorter events, 1.5 us)
Async XLA Ops:
  0.0 6.4 %copy-start = (bf16[512,144]{0,1:T(8,128)(2,1)S(1)}, bf16[512,144]{0,1:T(8,128)(2,1)}, u32[]{:S(2)}) copy-start(bf16[512,144]{0,1:T(8,128)(2,1)} %param.17) | copy-start | bytes 442372
  0.0 34.5 %collective-permute-start.1 = (bf16[80,3072]{1,0:T(8,128)(2,1)}, bf16[80,3072]{1,0:T(8,128)(2,1)S(1)}, u32[]{:S(2)}, u32[]{:S(2)}) collective-permute-start(bf16[80,3072]{1,0:T(8,128)(2,1)} %c0.1), channel_id=1, source_target_pairs={{0,2},{2,4},{4,6},{6,0},{1,3},{3,5},{5,7},{7,1},{8,10},{10,12},{12... | collective-permute-start | bytes 1474568 | tf_op jit(solution)/shard_map/ppermute | solution.py:32
  1.6 33.0 %collective-permute-start.2 = (bf16[80,3072]{1,0:T(8,128)(2,1)}, bf16[80,3072]{1,0:T(8,128)(2,1)S(1)}, u32[]{:S(2)}, u32[]{:S(2)}) collective-permute-start(bf16[80,3072]{1,0:T(8,128)(2,1)} %c0.1), channel_id=1, source_target_pairs={{0,6},{2,0},{4,2},{6,4},{1,7},{3,1},{5,3},{7,5},{8,14},{10,8},{12,... | collective-permute-start | bytes 1474568 | tf_op jit(solution)/shard_map/ppermute | solution.py:32
  3.2 31.9 %collective-permute-start.3 = (bf16[80,3072]{1,0:T(8,128)(2,1)}, bf16[80,3072]{1,0:T(8,128)(2,1)S(1)}, u32[]{:S(2)}, u32[]{:S(2)}) collective-permute-start(bf16[80,3072]{1,0:T(8,128)(2,1)} %c0.1), channel_id=1, source_target_pairs={{0,4},{2,6},{4,0},{6,2},{1,5},{3,7},{5,1},{7,3},{8,12},{10,14},{12... | collective-permute-start | bytes 1474568 | tf_op jit(solution)/shard_map/ppermute | solution.py:32
  5.1 31.0 %collective-permute-start.4 = (bf16[80,3072]{1,0:T(8,128)(2,1)}, bf16[80,3072]{1,0:T(8,128)(2,1)S(1)}, u32[]{:S(2)}, u32[]{:S(2)}) collective-permute-start(bf16[80,3072]{1,0:T(8,128)(2,1)} %c0.1), channel_id=1, source_target_pairs={{0,1},{1,0},{2,3},{3,2},{4,5},{5,4},{6,7},{7,6},{8,9},{9,8},{10,11... | collective-permute-start | bytes 1474568 | tf_op jit(solution)/shard_map/ppermute | solution.py:44
  5.1 74.0 %collective-permute-start = (bf16[384,3072]{1,0:T(8,128)(2,1)}, bf16[384,3072]{1,0:T(8,128)(2,1)}, u32[]{:S(2)}, u32[]{:S(2)}) collective-permute-start(bf16[384,3072]{1,0:T(8,128)(2,1)} %w_here.1), channel_id=1, source_target_pairs={{0,1},{1,0},{2,3},{3,2},{4,5},{5,4},{6,7},{7,6},{8,9},{9,8},{10,11... | collective-permute-start | bytes 7077896 | tf_op jit(solution)/shard_map/ppermute | solution.py:44
  7.3 15.8 %all-to-all-start = ((f32[16,3,128]{2,1,0:T(4,128)}), f32[16,3,128]{2,1,0:T(4,128)S(1)}, u32[]{:S(2)}, u32[]{:S(2)}) async-start(f32[16,3,128]{2,1,0:T(4,128)} %broadcast_in_dim.120), calls=%async_computation | async-start | bytes 65536 | tf_op jit(solution)/shard_map/all_to_all | solution.py:519
  16.7 17.3 %copy-start.21 = (s32[4]{0:T(128)}, s32[4]{0:T(128)S(1)}, u32[]{:S(2)}) copy-start(s32[4]{0:T(128)S(1)} %get-tuple-element.61) | copy-start | bytes 52
  17.6 16.4 %copy-start.24 = (s32[8]{0:T(128)}, s32[8]{0:T(128)S(1)}, u32[]{:S(2)}) copy-start(s32[8]{0:T(128)S(1)} %select_reduce_fusion) | copy-start | bytes 100
  23.8 10.2 %all-to-all-start.1 = ((f32[8,16,3,128]{3,1,2,0:T(8,128)}), f32[8,16,3,128]{3,1,2,0:T(8,128)S(1)}, u32[]{:S(2)}, u32[]{:S(2)}) async-start(f32[8,16,3,128]{3,1,2,0:T(8,128)} %broadcast_in_dim.121), calls=%async_computation.1 | async-start | bytes 393216 | tf_op jit(solution)/shard_map/all_to_all | solution.py:522
  34.5 4.2 %copy-start.8 = (bf16[80,3072]{1,0:T(8,128)(2,1)}, bf16[80,3072]{1,0:T(8,128)(2,1)S(1)}, u32[]{:S(2)}) copy-start(bf16[80,3072]{1,0:T(8,128)(2,1)S(1)} %collective-permute-done.1.c1) | copy-start | bytes 1474564
  34.5 1.9 %collective-permute-start.5 = (bf16[80,3072]{1,0:T(8,128)(2,1)S(1)}, bf16[80,3072]{1,0:T(8,128)(2,1)S(1)}, u32[]{:S(2)}, u32[]{:S(2)}) collective-permute-start(bf16[80,3072]{1,0:T(8,128)(2,1)S(1)} %collective-permute-done.1.c1), channel_id=1, source_target_pairs={{0,1},{1,0},{2,3},{3,2},{4,5},{5,4},{6,7},{7,6},{8,9},{9,8},{10,11... | collective-permute-start | bytes 1474568 | tf_op jit(solution)/shard_map/ppermute | solution.py:44
  34.6 3.2 %copy-start.9 = (bf16[80,3072]{1,0:T(8,128)(2,1)}, bf16[80,3072]{1,0:T(8,128)(2,1)S(1)}, u32[]{:S(2)}) copy-start(bf16[80,3072]{1,0:T(8,128)(2,1)S(1)} %collective-permute-done.2.c2) | copy-start | bytes 1474564
  34.6 2.5 %collective-permute-start.6 = (bf16[80,3072]{1,0:T(8,128)(2,1)S(1)}, bf16[80,3072]{1,0:T(8,128)(2,1)S(1)}, u32[]{:S(2)}, u32[]{:S(2)}) collective-permute-start(bf16[80,3072]{1,0:T(8,128)(2,1)S(1)} %collective-permute-done.2.c2), channel_id=1, source_target_pairs={{0,1},{1,0},{2,3},{3,2},{4,5},{5,4},{6,7},{7,6},{8,9},{9,8},{10,11... | collective-permute-start | bytes 1474568 | tf_op jit(solution)/shard_map/ppermute | solution.py:44
  35.1 2.8 %copy-start.10 = (bf16[80,3072]{1,0:T(8,128)(2,1)}, bf16[80,3072]{1,0:T(8,128)(2,1)S(1)}, u32[]{:S(2)}) copy-start(bf16[80,3072]{1,0:T(8,128)(2,1)S(1)} %collective-permute-done.3.c3) | copy-start | bytes 1474564
  35.1 2.7 %collective-permute-start.7 = (bf16[80,3072]{1,0:T(8,128)(2,1)S(1)}, bf16[80,3072]{1,0:T(8,128)(2,1)S(1)}, u32[]{:S(2)}, u32[]{:S(2)}) collective-permute-start(bf16[80,3072]{1,0:T(8,128)(2,1)S(1)} %collective-permute-done.3.c3), channel_id=1, source_target_pairs={{0,1},{1,0},{2,3},{3,2},{4,5},{5,4},{6,7},{7,6},{8,9},{9,8},{10,11... | collective-permute-start | bytes 1474568 | tf_op jit(solution)/shard_map/ppermute | solution.py:44
  36.2 1.7 copy-start.11
  36.5 2.2 %copy-start.12 = (bf16[80,3072]{1,0:T(8,128)(2,1)}, bf16[80,3072]{1,0:T(8,128)(2,1)S(1)}, u32[]{:S(2)}) copy-start(bf16[80,3072]{1,0:T(8,128)(2,1)S(1)} %collective-permute-done.5.c5) | copy-start | bytes 1474564
  37.2 0.8 copy-start.13
  37.9 0.8 copy-start.14
  38.7 40.5 %copy-start.3 = (bf16[384,3072]{1,0:T(8,128)(2,1)S(1)}, bf16[384,3072]{1,0:T(8,128)(2,1)}, u32[]{:S(2)}) copy-start(bf16[384,3072]{1,0:T(8,128)(2,1)} %w_here.1) | copy-start | bytes 7077892
  56.4 20.0 %collective-permute-start.8 = (bf16[2880,128]{1,0:T(8,128)(2,1)}, bf16[2880,128]{1,0:T(8,128)(2,1)S(1)}, u32[]{:S(2)}, u32[]{:S(2)}) collective-permute-start(bf16[2880,128]{1,0:T(8,128)(2,1)} %get-tuple-element.21.refs_0_.refs_3_.refs_1_), channel_id=1, source_target_pairs={{0,16},{16,32},{32,48},{48,0},{1,17},{17,33},{33,49},{49,1},{2,18}... | collective-permute-start | bytes 2211848 | tf_op jit(solution)/shard_map/ppermute | solution.py:36
  57.1 19.3 %collective-permute-start.9 = (bf16[2880,128]{1,0:T(8,128)(2,1)}, bf16[2880,128]{1,0:T(8,128)(2,1)S(1)}, u32[]{:S(2)}, u32[]{:S(2)}) collective-permute-start(bf16[2880,128]{1,0:T(8,128)(2,1)} %get-tuple-element.21.refs_0_.refs_3_.refs_1_), channel_id=1, source_target_pairs={{0,48},{16,0},{32,16},{48,32},{1,49},{17,1},{33,17},{49,33},{2,50}... | collective-permute-start | bytes 2211848 | tf_op jit(solution)/shard_map/ppermute | solution.py:36
  59.7 19.4 %collective-permute-start.10 = (bf16[2880,128]{1,0:T(8,128)(2,1)}, bf16[2880,128]{1,0:T(8,128)(2,1)S(1)}, u32[]{:S(2)}, u32[]{:S(2)}) collective-permute-start(bf16[2880,128]{1,0:T(8,128)(2,1)} %get-tuple-element.22.refs_3_.refs_4_.refs_0_), channel_id=1, source_target_pairs={{0,64},{64,8},{8,72},{72,0},{1,65},{65,9},{9,73},{73,1},{2,66},{66... | collective-permute-start | bytes 2211848 | tf_op jit(solution)/shard_map/ppermute | solution.py:40
  60.4 18.7 %collective-permute-start.11 = (bf16[2880,128]{1,0:T(8,128)(2,1)}, bf16[2880,128]{1,0:T(8,128)(2,1)S(1)}, u32[]{:S(2)}, u32[]{:S(2)}) collective-permute-start(bf16[2880,128]{1,0:T(8,128)(2,1)} %get-tuple-element.22.refs_3_.refs_4_.refs_0_), channel_id=1, source_target_pairs={{0,72},{64,0},{8,64},{72,8},{1,73},{65,1},{9,65},{73,9},{2,74},{66... | collective-permute-start | bytes 2211848 | tf_op jit(solution)/shard_map/ppermute | solution.py:40
  63.6 22.4 %copy-start.20 = (s32[8]{0:T(128)}, s32[8]{0:T(128)S(1)}, u32[]{:S(2)}) copy-start(s32[8]{0:T(128)S(1)} %subtract_clamp_fusion.limits) | copy-start | bytes 100
  76.4 10.2 %copy-start.1 = (bf16[2880,128]{1,0:T(8,128)(2,1)}, bf16[2880,128]{1,0:T(8,128)(2,1)S(1)}, u32[]{:S(2)}) copy-start(bf16[2880,128]{1,0:T(8,128)(2,1)S(1)} %collective-permute-done.8.refs_1_.refs_4_.refs_2_) | copy-start | bytes 2211844
  76.4 10.2 %copy-start.2 = (bf16[2880,128]{1,0:T(8,128)(2,1)}, bf16[2880,128]{1,0:T(8,128)(2,1)S(1)}, u32[]{:S(2)}) copy-start(bf16[2880,128]{1,0:T(8,128)(2,1)S(1)} %collective-permute-done.9.refs_2_.refs_5_.refs_3_) | copy-start | bytes 2211844
  79.1 3.3 %copy-start.4 = (bf16[2880,128]{1,0:T(8,128)(2,1)}, bf16[2880,128]{1,0:T(8,128)(2,1)S(1)}, u32[]{:S(2)}) copy-start(bf16[2880,128]{1,0:T(8,128)(2,1)S(1)} %collective-permute-done.10.refs_4_.refs_5_.refs_0_) | copy-start | bytes 2211844
  79.1 4.3 %copy-start.5 = (bf16[2880,128]{1,0:T(8,128)(2,1)}, bf16[2880,128]{1,0:T(8,128)(2,1)S(1)}, u32[]{:S(2)}) copy-start(bf16[2880,128]{1,0:T(8,128)(2,1)S(1)} %collective-permute-done.11.refs_5_.refs_6_.refs_1_) | copy-start | bytes 2211844
  79.1 56.9 %collective-permute-start.23 = (bf16[384,3072]{1,0:T(8,128)(2,1)S(1)}, bf16[384,3072]{1,0:T(8,128)(2,1)}, u32[]{:S(2)}, u32[]{:S(2)}) collective-permute-start(bf16[384,3072]{1,0:T(8,128)(2,1)S(1)} %copy-done.3), channel_id=1, source_target_pairs={{0,2},{2,4},{4,6},{6,0},{1,3},{3,5},{5,7},{7,1},{8,10},{10,12},{12... | collective-permute-start | bytes 7077896 | tf_op jit(solution)/shard_map/ppermute | solution.py:32
  79.8 57.0 %collective-permute-start.25 = (bf16[384,3072]{1,0:T(8,128)(2,1)S(1)}, bf16[384,3072]{1,0:T(8,128)(2,1)}, u32[]{:S(2)}, u32[]{:S(2)}) collective-permute-start(bf16[384,3072]{1,0:T(8,128)(2,1)S(1)} %copy-done.3), channel_id=1, source_target_pairs={{0,6},{2,0},{4,2},{6,4},{1,7},{3,1},{5,3},{7,5},{8,14},{10,8},{12,... | collective-permute-start | bytes 7077896 | tf_op jit(solution)/shard_map/ppermute | solution.py:32
  82.5 18.3 %collective-permute-start.12 = (bf16[2880,128]{1,0:T(8,128)(2,1)}, bf16[2880,128]{1,0:T(8,128)(2,1)}, u32[]{:S(2)}, u32[]{:S(2)}) collective-permute-start(bf16[2880,128]{1,0:T(8,128)(2,1)} %get-tuple-element.21.refs_0_.refs_3_.refs_1_), channel_id=1, source_target_pairs={{0,32},{16,48},{32,0},{48,16},{1,33},{17,49},{33,1},{49,17},{2,34}... | collective-permute-start | bytes 2211848 | tf_op jit(solution)/shard_map/ppermute | solution.py:36
  83.4 18.0 %collective-permute-start.13 = (bf16[2880,128]{1,0:T(8,128)(2,1)}, bf16[2880,128]{1,0:T(8,128)(2,1)}, u32[]{:S(2)}, u32[]{:S(2)}) collective-permute-start(bf16[2880,128]{1,0:T(8,128)(2,1)} %get-tuple-element.22.refs_3_.refs_4_.refs_0_), channel_id=1, source_target_pairs={{0,8},{64,72},{8,0},{72,64},{1,9},{65,73},{9,1},{73,65},{2,10},{66... | collective-permute-start | bytes 2211848 | tf_op jit(solution)/shard_map/ppermute | solution.py:40
  99.5 19.4 %copy-start.25 = (s32[4]{0:T(128)S(1)}, s32[4]{0:T(128)}, u32[]{:S(2)}) copy-start(s32[4]{0:T(128)} %get-tuple-element.55) | copy-start | bytes 52
  99.5 19.4 %copy-start.26 = (s32[4]{0:T(128)S(1)}, s32[4]{0:T(128)}, u32[]{:S(2)}) copy-start(s32[4]{0:T(128)} %get-tuple-element.56) | copy-start | bytes 52
  99.5 20.0 %copy-start.22 = (s32[4]{0:T(128)S(1)}, s32[4]{0:T(128)}, u32[]{:S(2)}) copy-start(s32[4]{0:T(128)} %copy-done.21) | copy-start | bytes 52
  99.5 20.1 %copy-start.23 = (s32[4]{0:T(128)S(1)}, s32[4]{0:T(128)}, u32[]{:S(2)}) copy-start(s32[4]{0:T(128)} %get-tuple-element.40) | copy-start | bytes 52
  111.7 22.3 %collective-permute-start.14 = (bf16[208,640]{1,0:T(8,128)(2,1)}, bf16[208,640]{1,0:T(8,128)(2,1)S(1)}, u32[]{:S(2)}, u32[]{:S(2)}) collective-permute-start(bf16[208,640]{1,0:T(8,128)(2,1)} %get-tuple-element.25), channel_id=1, source_target_pairs={{0,48},{16,0},{32,16},{48,32},{1,49},{17,1},{33,17},{49,33},{2,50}... | collective-permute-start | bytes 798728 | tf_op jit(solution)/shard_map/ppermute | solution.py:36
  117.4 16.7 %collective-permute-start.15 = (bf16[208,640]{1,0:T(8,128)(2,1)}, bf16[208,640]{1,0:T(8,128)(2,1)S(1)}, u32[]{:S(2)}, u32[]{:S(2)}) collective-permute-start(bf16[208,640]{1,0:T(8,128)(2,1)} %get-tuple-element.26), channel_id=1, source_target_pairs={{0,16},{16,32},{32,48},{48,0},{1,17},{17,33},{33,49},{49,1},{2,18}... | collective-permute-start | bytes 798728 | tf_op jit(solution)/shard_map/ppermute | solution.py:36
  117.4 18.7 %collective-permute-start.16 = (bf16[208,640]{1,0:T(8,128)(2,1)}, bf16[208,640]{1,0:T(8,128)(2,1)S(1)}, u32[]{:S(2)}, u32[]{:S(2)}) collective-permute-start(bf16[208,640]{1,0:T(8,128)(2,1)} %get-tuple-element.27), channel_id=1, source_target_pairs={{0,32},{16,48},{32,0},{48,16},{1,33},{17,49},{33,1},{49,17},{2,34}... | collective-permute-start | bytes 798728 | tf_op jit(solution)/shard_map/ppermute | solution.py:36
  134.0 2.2 %copy-start.15 = (bf16[208,640]{1,0:T(8,128)(2,1)}, bf16[208,640]{1,0:T(8,128)(2,1)S(1)}, u32[]{:S(2)}) copy-start(bf16[208,640]{1,0:T(8,128)(2,1)S(1)} %collective-permute-done.14.a1) | copy-start | bytes 798724
  134.0 9.2 %collective-permute-start.17 = (bf16[208,640]{1,0:T(8,128)(2,1)}, bf16[208,640]{1,0:T(8,128)(2,1)}, u32[]{:S(2)}, u32[]{:S(2)}) collective-permute-start(bf16[208,640]{1,0:T(8,128)(2,1)} %get-tuple-element.29), channel_id=1, source_target_pairs={{0,72},{64,0},{8,64},{72,8},{1,73},{65,1},{9,65},{73,9},{2,74},{66... | collective-permute-start | bytes 798728 | tf_op jit(solution)/shard_map/ppermute | solution.py:40
  134.1 2.1 %copy-start.16 = (bf16[208,640]{1,0:T(8,128)(2,1)}, bf16[208,640]{1,0:T(8,128)(2,1)S(1)}, u32[]{:S(2)}) copy-start(bf16[208,640]{1,0:T(8,128)(2,1)S(1)} %collective-permute-done.15.a2) | copy-start | bytes 798724
  134.1 12.2 %collective-permute-start.18 = (bf16[208,640]{1,0:T(8,128)(2,1)}, bf16[208,640]{1,0:T(8,128)(2,1)}, u32[]{:S(2)}, u32[]{:S(2)}) collective-permute-start(bf16[208,640]{1,0:T(8,128)(2,1)} %get-tuple-element.31), channel_id=1, source_target_pairs={{0,64},{64,8},{8,72},{72,0},{1,65},{65,9},{9,73},{73,1},{2,66},{66... | collective-permute-start | bytes 798728 | tf_op jit(solution)/shard_map/ppermute | solution.py:40
  136.1 0.7 copy-start.17
  136.1 10.2 %collective-permute-start.19 = (bf16[208,640]{1,0:T(8,128)(2,1)}, bf16[208,640]{1,0:T(8,128)(2,1)}, u32[]{:S(2)}, u32[]{:S(2)}) collective-permute-start(bf16[208,640]{1,0:T(8,128)(2,1)} %get-tuple-element.32), channel_id=1, source_target_pairs={{0,8},{64,72},{8,0},{72,64},{1,9},{65,73},{9,1},{73,65},{2,10},{66... | collective-permute-start | bytes 798728 | tf_op jit(solution)/shard_map/ppermute | solution.py:40
  136.1 23.6 %collective-permute-start.24 = (bf16[384,3072]{1,0:T(8,128)(2,1)}, bf16[384,3072]{1,0:T(8,128)(2,1)}, u32[]{:S(2)}, u32[]{:S(2)}) collective-permute-start(bf16[384,3072]{1,0:T(8,128)(2,1)} %collective-permute-done.23.refs_2_), channel_id=1, source_target_pairs={{0,1},{1,0},{2,3},{3,2},{4,5},{5,4},{6,7},{7,6},{8,9},{9,8},{10,11... | collective-permute-start | bytes 7077896 | tf_op jit(solution)/shard_map/ppermute | solution.py:44
  136.8 22.9 %collective-permute-start.26 = (bf16[384,3072]{1,0:T(8,128)(2,1)}, bf16[384,3072]{1,0:T(8,128)(2,1)S(1)}, u32[]{:S(2)}, u32[]{:S(2)}) collective-permute-start(bf16[384,3072]{1,0:T(8,128)(2,1)} %collective-permute-done.25.refs_4_), channel_id=1, source_target_pairs={{0,1},{1,0},{2,3},{3,2},{4,5},{5,4},{6,7},{7,6},{8,9},{9,8},{10,11... | collective-permute-start | bytes 7077896 | tf_op jit(solution)/shard_map/ppermute | solution.py:44
  149.7 1.7 collective-permute-start.20
  151.4 3.4 %copy-start.7 = (bf16[320,384]{1,0:T(8,128)(2,1)}, bf16[320,384]{1,0:T(8,128)(2,1)S(1)}, u32[]{:S(2)}) copy-start(bf16[320,384]{1,0:T(8,128)(2,1)S(1)} %collective-permute-done.20.theirs) | copy-start | bytes 737284
  151.4 8.2 %collective-permute-start.21 = (bf16[160,384]{1,0:T(8,128)(2,1)S(1)}, bf16[160,384]{1,0:T(8,128)(2,1)S(1)}, u32[]{:S(2)}, u32[]{:S(2)}) collective-permute-start(bf16[160,384]{1,0:T(8,128)(2,1)S(1)} %pad_maximum_fusion.1), channel_id=1, source_target_pairs={{0,2},{2,4},{4,6},{6,0},{1,3},{3,5},{5,7},{7,1},{8,10},{10,12},{12... | collective-permute-start | bytes 368648 | tf_op jit(solution)/shard_map/ppermute | solution.py:32
  151.6 8.1 %collective-permute-start.22 = (bf16[160,384]{1,0:T(8,128)(2,1)S(1)}, bf16[160,384]{1,0:T(8,128)(2,1)S(1)}, u32[]{:S(2)}, u32[]{:S(2)}) collective-permute-start(bf16[160,384]{1,0:T(8,128)(2,1)S(1)} %pad_maximum_fusion.2), channel_id=1, source_target_pairs={{0,6},{2,0},{4,2},{6,4},{1,7},{3,1},{5,3},{7,5},{8,14},{10,8},{12,... | collective-permute-start | bytes 368648 | tf_op jit(solution)/shard_map/ppermute | solution.py:32
  159.6 14.4 %collective-permute-start.27 = (bf16[80,3072]{1,0:T(8,128)(2,1)}, bf16[80,3072]{1,0:T(8,128)(2,1)S(1)}, u32[]{:S(2)}, u32[]{:S(2)}) collective-permute-start(bf16[80,3072]{1,0:T(8,128)(2,1)} %far_output.1), channel_id=1, source_target_pairs={{0,4},{2,6},{4,0},{6,2},{1,5},{3,7},{5,1},{7,3},{8,12},{10,14},{12... | collective-permute-start | bytes 1474568 | tf_op jit(solution)/shard_map/ppermute | solution.py:32
  159.7 0.7 copy-start.18
  159.7 0.7 copy-start.19
  160.4 1.4 copy-start.6
where the time goes:
time: 180 us; the launch traced here: 176 us
  Pallas kernels  76 us (42%)
  starting transfers between devices  44.1 us (24%)
  waiting for transfers between devices  34.6 us (19%)
  other arithmetic  13 us (7%)
  local copies, waits for them, and re-layouts  7.25 us (4%)
    pallas_call x4, Pallas kernels, attend(): pl.pallas_call(functools.partial(attend_kernel, places=places, n_k=n_k, c...  42.1 us
    pallas_call x1, Pallas kernels, project(): pl.pallas_call(project_kernel, out_shape=[jax.ShapeDtypeStruct((2880, 128...  17.8 us
    ppermute x6, waiting for transfers between devices, shift_z(): return lax.ppermute(value, 'z', [(i, (i + step) % 4) for i in range(4)])  14.1 us
    ppermute x8, starting transfers between devices, shift_x(): return lax.ppermute(value, 'x', [(i, (i + step) % 4) for i in range(4)])  11.8 us
    ppermute x6, starting transfers between devices, shift_z(): return lax.ppermute(value, 'z', [(i, (i + step) % 4) for i in range(4)])  11.5 us
    all_to_all x1, starting transfers between devices, local(): lax.all_to_all(jnp.broadcast_to(packed[None], (16, 3, 128)), tiles_axes,...  8.05 us
    pallas_call x1, Pallas kernels, near_output(): pl.pallas_call(near_output_kernel, out_shape=jax.ShapeDtypeStruct((OWN, D...  7.95 us
    ppermute x6, starting transfers between devices, shift_y(): lax.ppermute(value, Y_AXES, [(Y_INDEX[i], Y_INDEX[(i + step) % 4]) for i...  7.94 us
  transfers between devices with their start and end apart: 30, of which 12 were waited for; matrix products, arithmetic and copies ran while one was open for 8% of the time, Pallas kernels for 43%

commit v1 on v0

--- a/solution.py
+++ b/solution.py
@@ -546,7 +546,8 @@
     starts = jnp.concatenate([(x_ring * 2 + core) * OWN, (x_ring * 2 + 1 - core) * OWN])
     info = jnp.concatenate([starts, jnp.stack([piece, boundary])])
 
-    cos, sin = rope_tables(piece, boundary)
+    late_boundary, _ = lax.optimization_barrier((boundary, across[3]))
+    cos, sin = rope_tables(piece, late_boundary)
     along_z, along_y = project(
         info, chunks, modulation, w_query, w_key, w_value, cos, sin, gain_query[None, :],
         gain_key[None, :],

time: 180 us -> 182 us (1.011); the launches traced: 176 us -> 181 us
  waiting for transfers between devices: 34.6 us -> 40 us
    ppermute x6, waiting for transfers between devices: 14.1 us -> 18.8 us  [shift_z(): return lax.ppermute(value, 'z', [(i, (i + step) % 4) for i in range(4)])]
    ppermute x6, starting transfers between devices: 11.5 us -> 7.79 us  [shift_z(): return lax.ppermute(value, 'z', [(i, (i + step) % 4) for i in range(4)])]
    ppermute x6, starting transfers between devices: 7.94 us -> 11.4 us  [shift_y(): lax.ppermute(value, Y_AXES, [(Y_INDEX[i], Y_INDEX[(i + step) % 4]) for i...]
    all_to_all x1, waiting for transfers between devices: 1.26 us -> 4.42 us  [local(): lax.all_to_all(jnp.broadcast_to(packed[None], (16, 3, 128)), tiles_axes,...]
  transfers between devices with their start and end apart: 30 -> 30, of which waited for: 12 -> 10; matrix products, arithmetic and copies ran while one was open for 8% -> 8% of each run, Pallas kernels for 43% -> 42%
where the time goes in v1:
time: 182 us; the launch traced here: 181 us
  Pallas kernels  75 us (41%)
  starting transfers between devices  44.1 us (24%)
  waiting for transfers between devices  40 us (22%)
  other arithmetic  13 us (7%)
  local copies, waits for them, and re-layouts  7.1 us (4%)
    pallas_call x4, Pallas kernels, attend(): pl.pallas_call(functools.partial(attend_kernel, places=places, n_k=n_k, c...  41.1 us
    ppermute x6, waiting for transfers between devices, shift_z(): return lax.ppermute(value, 'z', [(i, (i + step) % 4) for i in range(4)])  18.8 us
    pallas_call x1, Pallas kernels, project(): pl.pallas_call(project_kernel, out_shape=[jax.ShapeDtypeStruct((2880, 128...  17.8 us
    ppermute x8, starting transfers between devices, shift_x(): return lax.ppermute(value, 'x', [(i, (i + step) % 4) for i in range(4)])  11.8 us
    ppermute x6, starting transfers between devices, shift_y(): lax.ppermute(value, Y_AXES, [(Y_INDEX[i], Y_INDEX[(i + step) % 4]) for i...  11.4 us
    all_to_all x1, starting transfers between devices, local(): lax.all_to_all(jnp.broadcast_to(packed[None], (16, 3, 128)), tiles_axes,...  8.05 us
    pallas_call x1, Pallas kernels, near_output(): pl.pallas_call(near_output_kernel, out_shape=jax.ShapeDtypeStruct((OWN, D...  7.95 us
    ppermute x6, starting transfers between devices, shift_z(): return lax.ppermute(value, 'z', [(i, (i + step) % 4) for i in range(4)])  7.79 us
  transfers between devices with their start and end apart: 30, of which 10 were waited for; matrix products, arithmetic and copies ran while one was open for 8% of the time, Pallas kernels for 42%

profile of v1, /device:TPU:0, one launch (start us, length us, event | category | flops | bytes accessed | tf_op | source)
XLA Modules:
  0.0 180.6 jit_solution(16757044501962900782)
XLA Ops:
  0.0 1.6 collective-permute-start.1
  1.6 1.7 collective-permute-start.2
  3.2 1.9 %collective-permute-start.3 = (bf16[80,3072]{1,0:T(8,128)(2,1)}, bf16[80,3072]{1,0:T(8,128)(2,1)S(1)}, u32[]{:S(2)}, u32[]{:S(2)}) collective-permute-start(bf16[80,3072]{1,0:T(8,128)(2,1)} %c0.1), channel_id=1, source_target_pairs={{0,4},{2,6},{4,0},{6,2},{1,5},{3,7},{5,1},{7,3},{8,12},{10,14},{12... | collective-permute-start | bytes 1474568 | tf_op jit(solution)/shard_map/ppermute | solution.py:32
  5.1 0.5 collective-permute-start
  5.7 0.7 convert_element_type.17
  6.3 0.1 multiply_cosine_fusion
  6.5 0.1 fusion.19
  6.7 0.6 broadcast_in_dim.120
  7.3 8.0 %all-to-all-start = ((f32[16,3,128]{2,1,0:T(4,128)}), f32[16,3,128]{2,1,0:T(4,128)S(1)}, u32[]{:S(2)}, u32[]{:S(2)}) async-start(f32[16,3,128]{2,1,0:T(4,128)} %broadcast_in_dim.120), calls=%async_computation | async-start | bytes 65536 | tf_op jit(solution)/shard_map/all_to_all | solution.py:519
  15.5 1.2 subtract_multiply_fusion.1
  16.8 0.8 select_reduce_fusion
  17.8 0.1 tile.7
  18.7 4.4 %all-to-all-done = f32[16,3,128]{2,1,0:T(4,128)S(1)} async-done(((f32[16,3,128]{2,1,0:T(4,128)}), f32[16,3,128]{2,1,0:T(4,128)S(1)}, u32[]{:S(2)}, u32[]{:S(2)}) %all-to-all-start) | async-done | bytes 24608 | tf_op jit(solution)/shard_map/all_to_all | solution.py:519
  23.1 0.7 broadcast_in_dim.121
  23.8 3.4 %all-to-all-start.1 = ((f32[8,16,3,128]{3,1,2,0:T(8,128)}), f32[8,16,3,128]{3,1,2,0:T(8,128)S(1)}, u32[]{:S(2)}, u32[]{:S(2)}) async-start(f32[8,16,3,128]{3,1,2,0:T(8,128)} %broadcast_in_dim.121), calls=%async_computation.1 | async-start | bytes 393216 | tf_op jit(solution)/shard_map/all_to_all | solution.py:522
  27.2 0.7 pad_add_fusion.2.info
  27.9 6.1 %all-to-all-done.1 = f32[8,16,3,128]{3,1,2,0:T(8,128)S(1)} async-done(((f32[8,16,3,128]{3,1,2,0:T(8,128)}), f32[8,16,3,128]{3,1,2,0:T(8,128)S(1)}, u32[]{:S(2)}, u32[]{:S(2)}) %all-to-all-start.1) | async-done | bytes 196640 | tf_op jit(solution)/shard_map/all_to_all | solution.py:522
  34.1 0.2 stack_reshape.6
  34.3 0.2 stack_reshape.7
  34.5 0.8 pad_maximum_fusion.mods
  35.3 0.5 collective-permute-start.5
  35.8 0.1 collective-permute-start.6
  36.1 3.0 %negate_select_fusion = (f32[640,128]{1,0:T(8,128)}, f32[640,128]{1,0:T(8,128)}) fusion(s32[128]{0:T(128)S(1)} %get-tuple-element.67, s32[128]{0:T(128)S(1)} %get-tuple-element.69, pred[640]{0:T(1024)(128)(4,1)S(1)} %fusion.13, pred[128]{0:T(512)(128)(4,1)S(1)} %get-tuple-element.65, f32[128]{0:T(128)S(1)} %mul.106, s32[640]{0:T(1024)S(1)} %fusion.15, ...), kind=kLoop, calls=%fused_computation.5 | loop fusion | flops 3031040 | bytes 676096 | tf_op jit(solution)/shard_map/jit(_where)/select_n | solution.py:76
  39.2 0.7 copy-done.11
  39.9 0.2 copy-done.13
  40.1 0.2 copy-done.14
  40.3 0.1 copy-done.12
  40.4 17.8 %project.1 = (bf16[2880,128]{1,0:T(8,128)(2,1)}, bf16[2880,128]{1,0:T(8,128)(2,1)}) custom-call(s32[10]{0:T(128)} %pad_add_fusion.2.info, bf16[80,3072]{1,0:T(8,128)(2,1)} %c0.1, bf16[80,3072]{1,0:T(8,128)(2,1)} %copy-done.8, bf16[80,3072]{1,0:T(8,128)(2,1)} %copy-done.9, bf16[80,3072]{1,0:T(8,128)(2,1)} %copy-done.10, bf16[80,3072]{1,0:T(8,128)(2,1)} %copy-done.11, ...), custom_call_target="tpu_custom_call" | custom-call | tf_op jit(solution)/shard_map/project/pallas_call | solution.py:180
  58.1 0.6 collective-permute-start.8
  58.8 2.7 %collective-permute-start.9 = (bf16[2880,128]{1,0:T(8,128)(2,1)}, bf16[2880,128]{1,0:T(8,128)(2,1)S(1)}, u32[]{:S(2)}, u32[]{:S(2)}) collective-permute-start(bf16[2880,128]{1,0:T(8,128)(2,1)} %get-tuple-element.23.refs_0_.refs_3_.refs_1_), channel_id=1, source_target_pairs={{0,48},{16,0},{32,16},{48,32},{1,49},{17,1},{33,17},{49,33},{2,50}... | collective-permute-start | bytes 2211848 | tf_op jit(solution)/shard_map/ppermute | solution.py:36
  61.5 0.6 collective-permute-start.10
  62.0 2.7 %collective-permute-start.11 = (bf16[2880,128]{1,0:T(8,128)(2,1)}, bf16[2880,128]{1,0:T(8,128)(2,1)S(1)}, u32[]{:S(2)}, u32[]{:S(2)}) collective-permute-start(bf16[2880,128]{1,0:T(8,128)(2,1)} %get-tuple-element.24.refs_3_.refs_4_.refs_0_), channel_id=1, source_target_pairs={{0,72},{64,0},{8,64},{72,8},{1,73},{65,1},{9,65},{73,9},{2,74},{66... | collective-permute-start | bytes 2211848 | tf_op jit(solution)/shard_map/ppermute | solution.py:40
  64.7 0.7 subtract_clamp_fusion.limits
  65.4 13.1 %collective-permute-done.8.refs_1_.refs_4_.refs_2_ = bf16[2880,128]{1,0:T(8,128)(2,1)S(1)} collective-permute-done((bf16[2880,128]{1,0:T(8,128)(2,1)}, bf16[2880,128]{1,0:T(8,128)(2,1)S(1)}, u32[]{:S(2)}, u32[]{:S(2)}) %collective-permute-start.8) | collective-permute-done | bytes 737312 | tf_op jit(solution)/shard_map/ppermute | solution.py:36
  78.5 2.7 %collective-permute-done.10.refs_4_.refs_5_.refs_0_ = bf16[2880,128]{1,0:T(8,128)(2,1)S(1)} collective-permute-done((bf16[2880,128]{1,0:T(8,128)(2,1)}, bf16[2880,128]{1,0:T(8,128)(2,1)S(1)}, u32[]{:S(2)}, u32[]{:S(2)}) %collective-permute-start.10) | collective-permute-done | bytes 737312 | tf_op jit(solution)/shard_map/ppermute | solution.py:40
  81.2 0.6 collective-permute-start.23
  81.8 2.7 %collective-permute-start.25 = (bf16[384,3072]{1,0:T(8,128)(2,1)S(1)}, bf16[384,3072]{1,0:T(8,128)(2,1)}, u32[]{:S(2)}, u32[]{:S(2)}) collective-permute-start(bf16[384,3072]{1,0:T(8,128)(2,1)S(1)} %copy-done.3), channel_id=1, source_target_pairs={{0,6},{2,0},{4,2},{6,4},{1,7},{3,1},{5,3},{7,5},{8,14},{10,8},{12,... | collective-permute-start | bytes 7077896 | tf_op jit(solution)/shard_map/ppermute | solution.py:32
  84.5 1.6 collective-permute-start.13
  86.0 0.6 fusion.46
  86.7 10.7 %near_a.1.refs_8_ = f32[3,3,80,640]{3,2,1,0:T(8,128)} custom-call(s32[8]{0:T(128)} %copy-done.20, bf16[2880,128]{1,0:T(8,128)(2,1)} %get-tuple-element.23.refs_0_.refs_3_.refs_1_, bf16[2880,128]{1,0:T(8,128)(2,1)} %copy-done.1, bf16[2880,128]{1,0:T(8,128)(2,1)} %copy-done.2, bf16[2880,128]{1,0:T(8,128)(2,1)} %get-tuple-element.24.refs_3_.refs_4_.refs_0_, ...), custom_call_target="tpu_custom_call" | custom-call | flops 1000 | bytes 1000 | tf_op jit(solution)/shard_map/near_a/pallas_call | solution.py:375
  97.4 5.7 %collective-permute-done.12.refs_3_.refs_6_.refs_4_ = bf16[2880,128]{1,0:T(8,128)(2,1)} collective-permute-done((bf16[2880,128]{1,0:T(8,128)(2,1)}, bf16[2880,128]{1,0:T(8,128)(2,1)}, u32[]{:S(2)}, u32[]{:S(2)}) %collective-permute-start.12) | collective-permute-done | bytes 737312 | tf_op jit(solution)/shard_map/ppermute | solution.py:36
  103.2 10.1 %far_a.1 = (f32[3,80,640]{2,1,0:T(8,128)}, bf16[208,640]{1,0:T(8,128)(2,1)}, bf16[208,640]{1,0:T(8,128)(2,1)}, bf16[208,640]{1,0:T(8,128)(2,1)}) custom-call(s32[8]{0:T(128)} %copy-done.20, bf16[2880,128]{1,0:T(8,128)(2,1)} %get-tuple-element.23.refs_0_.refs_3_.refs_1_, bf16[2880,128]{1,0:T(8,128)(2,1)} %copy-done.1, bf16[2880,128]{1,0:T(8,128)(2,1)} %copy-done.2, ...), custom_call_target="tpu_custom_call" | custom-call | flops 1000 | bytes 1000 | tf_op jit(solution)/shard_map/far_a/pallas_call | solution.py:375
  113.4 2.0 %collective-permute-start.15 = (bf16[208,640]{1,0:T(8,128)(2,1)}, bf16[208,640]{1,0:T(8,128)(2,1)S(1)}, u32[]{:S(2)}, u32[]{:S(2)}) collective-permute-start(bf16[208,640]{1,0:T(8,128)(2,1)} %get-tuple-element.28), channel_id=1, source_target_pairs={{0,16},{16,32},{32,48},{48,0},{1,17},{17,33},{33,49},{49,1},{2,18}... | collective-permute-start | bytes 798728 | tf_op jit(solution)/shard_map/ppermute | solution.py:36
  115.4 2.5 %collective-permute-start.16 = (bf16[208,640]{1,0:T(8,128)(2,1)}, bf16[208,640]{1,0:T(8,128)(2,1)S(1)}, u32[]{:S(2)}, u32[]{:S(2)}) collective-permute-start(bf16[208,640]{1,0:T(8,128)(2,1)} %get-tuple-element.29), channel_id=1, source_target_pairs={{0,32},{16,48},{32,0},{48,16},{1,33},{17,49},{33,1},{49,17},{2,34}... | collective-permute-start | bytes 798728 | tf_op jit(solution)/shard_map/ppermute | solution.py:36
  117.8 0.7 pad_add_fusion.3.limits
  118.5 0.5 add_multiply_fusion
  119.0 15.1 %rest_b.1 = (bf16[208,640]{1,0:T(8,128)(2,1)}, bf16[208,640]{1,0:T(8,128)(2,1)}, bf16[208,640]{1,0:T(8,128)(2,1)}) custom-call(s32[8]{0:T(128)} %pad_add_fusion.3.limits, bf16[2880,128]{1,0:T(8,128)(2,1)} %copy-done.4, bf16[2880,128]{1,0:T(8,128)(2,1)} %copy-done.5, bf16[2880,128]{1,0:T(8,128)(2,1)} %collective-permute-done.13.refs_7_.refs_2_, ...), custom_call_target="tpu_custom_call" | custom-call | flops 1000 | bytes 1000 | tf_op jit(solution)/shard_map/rest_b/pallas_call | solution.py:375
  134.2 5.1 %collective-permute-start.17 = (bf16[208,640]{1,0:T(8,128)(2,1)}, bf16[208,640]{1,0:T(8,128)(2,1)}, u32[]{:S(2)}, u32[]{:S(2)}) collective-permute-start(bf16[208,640]{1,0:T(8,128)(2,1)} %get-tuple-element.31), channel_id=1, source_target_pairs={{0,72},{64,0},{8,64},{72,8},{1,73},{65,1},{9,65},{73,9},{2,74},{66... | collective-permute-start | bytes 798728 | tf_op jit(solution)/shard_map/ppermute | solution.py:40
  139.3 1.5 collective-permute-start.19
  140.9 0.6 collective-permute-start.26
  141.5 1.2 pad_add_fusion.1.order
  142.7 5.1 %own_b.1 = f32[3,80,640]{2,1,0:T(8,128)} custom-call(s32[8]{0:T(128)} %pad_add_fusion.3.limits, bf16[2880,128]{1,0:T(8,128)(2,1)} %get-tuple-element.24.refs_3_.refs_4_.refs_0_, bf16[2880,128]{1,0:T(8,128)(2,1)} %get-tuple-element.23.refs_0_.refs_3_.refs_1_, bf16[2880,128]{1,0:T(8,128)(2,1)} %copy-done.1, bf16[2880,128]{1,0:T(8,128)(2,1)} %copy-done.2, ...), custom_call_target="tpu_custom_call" | custom-call | flops 1000 | bytes 1000 | tf_op jit(solution)/shard_map/own_b/pallas_call | solution.py:375
  147.8 0.5 collective-permute-done.17.b1
  148.3 2.3 %collective-permute-done.18.b2 = bf16[208,640]{1,0:T(8,128)(2,1)} collective-permute-done((bf16[208,640]{1,0:T(8,128)(2,1)}, bf16[208,640]{1,0:T(8,128)(2,1)}, u32[]{:S(2)}, u32[]{:S(2)}) %collective-permute-start.18) | collective-permute-done | bytes 266272 | tf_op jit(solution)/shard_map/ppermute | solution.py:40
  150.6 3.4 %merge.1 = (bf16[320,384]{1,0:T(8,128)(2,1)}, bf16[320,384]{1,0:T(8,128)(2,1)}) custom-call(s32[8]{0:T(128)} %pad_add_fusion.1.order, f32[3,80,640]{2,1,0:T(8,128)} %get-tuple-element.26.own_a, bf16[208,640]{1,0:T(8,128)(2,1)} %copy-done.15, bf16[208,640]{1,0:T(8,128)(2,1)} %copy-done.16, bf16[208,640]{1,0:T(8,128)(2,1)} %copy-done.17, f32[3,80,640]{2,1,0:T(8,128)} %own_b.1, ...), custom_call_target="tpu_custom_call" | custom-call | tf_op jit(solution)/shard_map/merge/pallas_call | solution.py:421
  154.0 0.9 fusion.41
  154.9 0.8 collective-permute-done.20.theirs
  155.9 3.3 %collective-permute-start.22 = (bf16[160,384]{1,0:T(8,128)(2,1)S(1)}, bf16[160,384]{1,0:T(8,128)(2,1)S(1)}, u32[]{:S(2)}, u32[]{:S(2)}) collective-permute-start(bf16[160,384]{1,0:T(8,128)(2,1)S(1)} %pad_maximum_fusion.2), channel_id=1, source_target_pairs={{0,6},{2,0},{4,2},{6,4},{1,7},{3,1},{5,3},{7,5},{8,14},{10,8},{12,... | collective-permute-start | bytes 368648 | tf_op jit(solution)/shard_map/ppermute | solution.py:32
  159.1 4.8 %far_output.1 = bf16[80,3072]{1,0:T(8,128)(2,1)} custom-call(bf16[320,384]{1,0:T(8,128)(2,1)} %get-tuple-element.35.mine, bf16[320,384]{1,0:T(8,128)(2,1)} %copy-done.7, bf16[384,3072]{1,0:T(8,128)(2,1)} %w_here.1, bf16[384,3072]{1,0:T(8,128)(2,1)} %collective-permute-done.refs_1_.w_other), custom_call_target="tpu_custom_call" | custom-call | flops 1000 | bytes 1000 | tf_op jit(solution)/shard_map/far_output/pallas_call | solution.py:447
  164.0 0.6 copy-done.18
  164.7 1.4 copy-done.6
  166.1 7.9 %near_output.1 = f32[80,3072]{1,0:T(8,128)} custom-call(bf16[320,384]{1,0:T(8,128)(2,1)} %get-tuple-element.35.mine, bf16[320,384]{1,0:T(8,128)(2,1)} %copy-done.7, bf16[160,384]{1,0:T(8,128)(2,1)} %copy-done.18, bf16[160,384]{1,0:T(8,128)(2,1)} %copy-done.19, bf16[384,3072]{1,0:T(8,128)(2,1)} %w_here.1, ...), custom_call_target="tpu_custom_call" | custom-call | tf_op jit(solution)/shard_map/near_output/pallas_call | solution.py:477
  174.1 4.3 %collective-permute-done.27 = bf16[80,3072]{1,0:T(8,128)(2,1)S(1)} collective-permute-done((bf16[80,3072]{1,0:T(8,128)(2,1)}, bf16[80,3072]{1,0:T(8,128)(2,1)S(1)}, u32[]{:S(2)}, u32[]{:S(2)}) %collective-permute-start.27) | collective-permute-done | bytes 491552 | tf_op jit(solution)/shard_map/ppermute | solution.py:32
  178.4 2.3 %multiply_convert_fusion = bf16[80,3072]{1,0:T(8,128)(2,1)} fusion(f32[80,3072]{1,0:T(8,128)} %near_output.1, bf16[80,3072]{1,0:T(8,128)(2,1)S(1)} %collective-permute-done.27, f32[3072]{0:T(1024)S(1)} %bitcast.22, f32[3072]{0:T(1024)S(1)} %bitcast.24, f32[3072]{0:T(1024)S(1)} %bitcast.21, f32[3072]{0:T(1024)S(1)} %bitcast.23, pred[80]{0:T(512)(128)(4,1)S(1)} %fusion.36, ...), kind=kLoop, calls=%fused_computation | loop fusion | flops 1720320 | bytes 2015392 | tf_op jit(solution)/shard_map/convert_element_type | solution.py:589
  (112 shorter events, 1.2 us)
Async XLA Ops:
  0.0 6.4 %copy-start = (bf16[512,144]{0,1:T(8,128)(2,1)S(1)}, bf16[512,144]{0,1:T(8,128)(2,1)}, u32[]{:S(2)}) copy-start(bf16[512,144]{0,1:T(8,128)(2,1)} %param.17) | copy-start | bytes 442372
  0.0 35.3 %collective-permute-start.1 = (bf16[80,3072]{1,0:T(8,128)(2,1)}, bf16[80,3072]{1,0:T(8,128)(2,1)S(1)}, u32[]{:S(2)}, u32[]{:S(2)}) collective-permute-start(bf16[80,3072]{1,0:T(8,128)(2,1)} %c0.1), channel_id=1, source_target_pairs={{0,2},{2,4},{4,6},{6,0},{1,3},{3,5},{5,7},{7,1},{8,10},{10,12},{12... | collective-permute-start | bytes 1474568 | tf_op jit(solution)/shard_map/ppermute | solution.py:32
  1.6 34.2 %collective-permute-start.2 = (bf16[80,3072]{1,0:T(8,128)(2,1)}, bf16[80,3072]{1,0:T(8,128)(2,1)S(1)}, u32[]{:S(2)}, u32[]{:S(2)}) collective-permute-start(bf16[80,3072]{1,0:T(8,128)(2,1)} %c0.1), channel_id=1, source_target_pairs={{0,6},{2,0},{4,2},{6,4},{1,7},{3,1},{5,3},{7,5},{8,14},{10,8},{12,... | collective-permute-start | bytes 1474568 | tf_op jit(solution)/shard_map/ppermute | solution.py:32
  3.2 32.0 %collective-permute-start.3 = (bf16[80,3072]{1,0:T(8,128)(2,1)}, bf16[80,3072]{1,0:T(8,128)(2,1)S(1)}, u32[]{:S(2)}, u32[]{:S(2)}) collective-permute-start(bf16[80,3072]{1,0:T(8,128)(2,1)} %c0.1), channel_id=1, source_target_pairs={{0,4},{2,6},{4,0},{6,2},{1,5},{3,7},{5,1},{7,3},{8,12},{10,14},{12... | collective-permute-start | bytes 1474568 | tf_op jit(solution)/shard_map/ppermute | solution.py:32
  5.1 34.0 %collective-permute-start.4 = (bf16[80,3072]{1,0:T(8,128)(2,1)}, bf16[80,3072]{1,0:T(8,128)(2,1)S(1)}, u32[]{:S(2)}, u32[]{:S(2)}) collective-permute-start(bf16[80,3072]{1,0:T(8,128)(2,1)} %c0.1), channel_id=1, source_target_pairs={{0,1},{1,0},{2,3},{3,2},{4,5},{5,4},{6,7},{7,6},{8,9},{9,8},{10,11... | collective-permute-start | bytes 1474568 | tf_op jit(solution)/shard_map/ppermute | solution.py:44
  5.1 76.0 %collective-permute-start = (bf16[384,3072]{1,0:T(8,128)(2,1)}, bf16[384,3072]{1,0:T(8,128)(2,1)}, u32[]{:S(2)}, u32[]{:S(2)}) collective-permute-start(bf16[384,3072]{1,0:T(8,128)(2,1)} %w_here.1), channel_id=1, source_target_pairs={{0,1},{1,0},{2,3},{3,2},{4,5},{5,4},{6,7},{7,6},{8,9},{9,8},{10,11... | collective-permute-start | bytes 7077896 | tf_op jit(solution)/shard_map/ppermute | solution.py:44
  7.3 15.8 %all-to-all-start = ((f32[16,3,128]{2,1,0:T(4,128)}), f32[16,3,128]{2,1,0:T(4,128)S(1)}, u32[]{:S(2)}, u32[]{:S(2)}) async-start(f32[16,3,128]{2,1,0:T(4,128)} %broadcast_in_dim.120), calls=%async_computation | async-start | bytes 65536 | tf_op jit(solution)/shard_map/all_to_all | solution.py:519
  16.7 17.3 %copy-start.21 = (s32[4]{0:T(128)}, s32[4]{0:T(128)S(1)}, u32[]{:S(2)}) copy-start(s32[4]{0:T(128)S(1)} %get-tuple-element.63) | copy-start | bytes 52
  17.6 16.4 %copy-start.24 = (s32[8]{0:T(128)}, s32[8]{0:T(128)S(1)}, u32[]{:S(2)}) copy-start(s32[8]{0:T(128)S(1)} %select_reduce_fusion) | copy-start | bytes 100
  23.8 10.2 %all-to-all-start.1 = ((f32[8,16,3,128]{3,1,2,0:T(8,128)}), f32[8,16,3,128]{3,1,2,0:T(8,128)S(1)}, u32[]{:S(2)}, u32[]{:S(2)}) async-start(f32[8,16,3,128]{3,1,2,0:T(8,128)} %broadcast_in_dim.121), calls=%async_computation.1 | async-start | bytes 393216 | tf_op jit(solution)/shard_map/all_to_all | solution.py:522
  35.3 3.9 %copy-start.10 = (bf16[80,3072]{1,0:T(8,128)(2,1)}, bf16[80,3072]{1,0:T(8,128)(2,1)S(1)}, u32[]{:S(2)}) copy-start(bf16[80,3072]{1,0:T(8,128)(2,1)S(1)} %collective-permute-done.3.c3) | copy-start | bytes 1474564
  35.3 3.9 %collective-permute-start.7 = (bf16[80,3072]{1,0:T(8,128)(2,1)S(1)}, bf16[80,3072]{1,0:T(8,128)(2,1)S(1)}, u32[]{:S(2)}, u32[]{:S(2)}) collective-permute-start(bf16[80,3072]{1,0:T(8,128)(2,1)S(1)} %collective-permute-done.3.c3), channel_id=1, source_target_pairs={{0,1},{1,0},{2,3},{3,2},{4,5},{5,4},{6,7},{7,6},{8,9},{9,8},{10,11... | collective-permute-start | bytes 1474568 | tf_op jit(solution)/shard_map/ppermute | solution.py:44
  35.3 5.0 %copy-start.8 = (bf16[80,3072]{1,0:T(8,128)(2,1)}, bf16[80,3072]{1,0:T(8,128)(2,1)S(1)}, u32[]{:S(2)}) copy-start(bf16[80,3072]{1,0:T(8,128)(2,1)S(1)} %collective-permute-done.1.c1) | copy-start | bytes 1474564
  35.3 3.8 %collective-permute-start.5 = (bf16[80,3072]{1,0:T(8,128)(2,1)S(1)}, bf16[80,3072]{1,0:T(8,128)(2,1)S(1)}, u32[]{:S(2)}, u32[]{:S(2)}) collective-permute-start(bf16[80,3072]{1,0:T(8,128)(2,1)S(1)} %collective-permute-done.1.c1), channel_id=1, source_target_pairs={{0,1},{1,0},{2,3},{3,2},{4,5},{5,4},{6,7},{7,6},{8,9},{9,8},{10,11... | collective-permute-start | bytes 1474568 | tf_op jit(solution)/shard_map/ppermute | solution.py:44
  35.8 3.4 %copy-start.9 = (bf16[80,3072]{1,0:T(8,128)(2,1)}, bf16[80,3072]{1,0:T(8,128)(2,1)S(1)}, u32[]{:S(2)}) copy-start(bf16[80,3072]{1,0:T(8,128)(2,1)S(1)} %collective-permute-done.2.c2) | copy-start | bytes 1474564
  35.8 3.3 %collective-permute-start.6 = (bf16[80,3072]{1,0:T(8,128)(2,1)S(1)}, bf16[80,3072]{1,0:T(8,128)(2,1)S(1)}, u32[]{:S(2)}, u32[]{:S(2)}) collective-permute-start(bf16[80,3072]{1,0:T(8,128)(2,1)S(1)} %collective-permute-done.2.c2), channel_id=1, source_target_pairs={{0,1},{1,0},{2,3},{3,2},{4,5},{5,4},{6,7},{7,6},{8,9},{9,8},{10,11... | collective-permute-start | bytes 1474568 | tf_op jit(solution)/shard_map/ppermute | solution.py:44
  39.1 0.8 copy-start.11
  39.1 1.0 copy-start.13
  39.1 1.1 copy-start.14
  39.2 1.2 copy-start.12
  40.4 40.8 %copy-start.3 = (bf16[384,3072]{1,0:T(8,128)(2,1)S(1)}, bf16[384,3072]{1,0:T(8,128)(2,1)}, u32[]{:S(2)}) copy-start(bf16[384,3072]{1,0:T(8,128)(2,1)} %w_here.1) | copy-start | bytes 7077892
  58.1 20.3 %collective-permute-start.8 = (bf16[2880,128]{1,0:T(8,128)(2,1)}, bf16[2880,128]{1,0:T(8,128)(2,1)S(1)}, u32[]{:S(2)}, u32[]{:S(2)}) collective-permute-start(bf16[2880,128]{1,0:T(8,128)(2,1)} %get-tuple-element.23.refs_0_.refs_3_.refs_1_), channel_id=1, source_target_pairs={{0,16},{16,32},{32,48},{48,0},{1,17},{17,33},{33,49},{49,1},{2,18}... | collective-permute-start | bytes 2211848 | tf_op jit(solution)/shard_map/ppermute | solution.py:36
  58.8 19.7 %collective-permute-start.9 = (bf16[2880,128]{1,0:T(8,128)(2,1)}, bf16[2880,128]{1,0:T(8,128)(2,1)S(1)}, u32[]{:S(2)}, u32[]{:S(2)}) collective-permute-start(bf16[2880,128]{1,0:T(8,128)(2,1)} %get-tuple-element.23.refs_0_.refs_3_.refs_1_), channel_id=1, source_target_pairs={{0,48},{16,0},{32,16},{48,32},{1,49},{17,1},{33,17},{49,33},{2,50}... | collective-permute-start | bytes 2211848 | tf_op jit(solution)/shard_map/ppermute | solution.py:36
  61.5 19.7 %collective-permute-start.10 = (bf16[2880,128]{1,0:T(8,128)(2,1)}, bf16[2880,128]{1,0:T(8,128)(2,1)S(1)}, u32[]{:S(2)}, u32[]{:S(2)}) collective-permute-start(bf16[2880,128]{1,0:T(8,128)(2,1)} %get-tuple-element.24.refs_3_.refs_4_.refs_0_), channel_id=1, source_target_pairs={{0,64},{64,8},{8,72},{72,0},{1,65},{65,9},{9,73},{73,1},{2,66},{66... | collective-permute-start | bytes 2211848 | tf_op jit(solution)/shard_map/ppermute | solution.py:40
  62.0 19.1 %collective-permute-start.11 = (bf16[2880,128]{1,0:T(8,128)(2,1)}, bf16[2880,128]{1,0:T(8,128)(2,1)S(1)}, u32[]{:S(2)}, u32[]{:S(2)}) collective-permute-start(bf16[2880,128]{1,0:T(8,128)(2,1)} %get-tuple-element.24.refs_3_.refs_4_.refs_0_), channel_id=1, source_target_pairs={{0,72},{64,0},{8,64},{72,8},{1,73},{65,1},{9,65},{73,9},{2,74},{66... | collective-permute-start | bytes 2211848 | tf_op jit(solution)/shard_map/ppermute | solution.py:40
  65.4 20.7 %copy-start.20 = (s32[8]{0:T(128)}, s32[8]{0:T(128)S(1)}, u32[]{:S(2)}) copy-start(s32[8]{0:T(128)S(1)} %subtract_clamp_fusion.limits) | copy-start | bytes 100
  78.5 8.2 %copy-start.1 = (bf16[2880,128]{1,0:T(8,128)(2,1)}, bf16[2880,128]{1,0:T(8,128)(2,1)S(1)}, u32[]{:S(2)}) copy-start(bf16[2880,128]{1,0:T(8,128)(2,1)S(1)} %collective-permute-done.8.refs_1_.refs_4_.refs_2_) | copy-start | bytes 2211844
  78.5 8.2 %copy-start.2 = (bf16[2880,128]{1,0:T(8,128)(2,1)}, bf16[2880,128]{1,0:T(8,128)(2,1)S(1)}, u32[]{:S(2)}) copy-start(bf16[2880,128]{1,0:T(8,128)(2,1)S(1)} %collective-permute-done.9.refs_2_.refs_5_.refs_3_) | copy-start | bytes 2211844
  81.1 3.3 %copy-start.4 = (bf16[2880,128]{1,0:T(8,128)(2,1)}, bf16[2880,128]{1,0:T(8,128)(2,1)S(1)}, u32[]{:S(2)}) copy-start(bf16[2880,128]{1,0:T(8,128)(2,1)S(1)} %collective-permute-done.10.refs_4_.refs_5_.refs_0_) | copy-start | bytes 2211844
  81.1 3.3 %copy-start.5 = (bf16[2880,128]{1,0:T(8,128)(2,1)}, bf16[2880,128]{1,0:T(8,128)(2,1)S(1)}, u32[]{:S(2)}) copy-start(bf16[2880,128]{1,0:T(8,128)(2,1)S(1)} %collective-permute-done.11.refs_5_.refs_6_.refs_1_) | copy-start | bytes 2211844
  81.2 59.7 %collective-permute-start.23 = (bf16[384,3072]{1,0:T(8,128)(2,1)S(1)}, bf16[384,3072]{1,0:T(8,128)(2,1)}, u32[]{:S(2)}, u32[]{:S(2)}) collective-permute-start(bf16[384,3072]{1,0:T(8,128)(2,1)S(1)} %copy-done.3), channel_id=1, source_target_pairs={{0,2},{2,4},{4,6},{6,0},{1,3},{3,5},{5,7},{7,1},{8,10},{10,12},{12... | collective-permute-start | bytes 7077896 | tf_op jit(solution)/shard_map/ppermute | solution.py:32
  81.8 59.1 %collective-permute-start.25 = (bf16[384,3072]{1,0:T(8,128)(2,1)S(1)}, bf16[384,3072]{1,0:T(8,128)(2,1)}, u32[]{:S(2)}, u32[]{:S(2)}) collective-permute-start(bf16[384,3072]{1,0:T(8,128)(2,1)S(1)} %copy-done.3), channel_id=1, source_target_pairs={{0,6},{2,0},{4,2},{6,4},{1,7},{3,1},{5,3},{7,5},{8,14},{10,8},{12,... | collective-permute-start | bytes 7077896 | tf_op jit(solution)/shard_map/ppermute | solution.py:32
  84.5 18.7 %collective-permute-start.12 = (bf16[2880,128]{1,0:T(8,128)(2,1)}, bf16[2880,128]{1,0:T(8,128)(2,1)}, u32[]{:S(2)}, u32[]{:S(2)}) collective-permute-start(bf16[2880,128]{1,0:T(8,128)(2,1)} %get-tuple-element.23.refs_0_.refs_3_.refs_1_), channel_id=1, source_target_pairs={{0,32},{16,48},{32,0},{48,16},{1,33},{17,49},{33,1},{49,17},{2,34}... | collective-permute-start | bytes 2211848 | tf_op jit(solution)/shard_map/ppermute | solution.py:36
  84.5 18.7 %collective-permute-start.13 = (bf16[2880,128]{1,0:T(8,128)(2,1)}, bf16[2880,128]{1,0:T(8,128)(2,1)}, u32[]{:S(2)}, u32[]{:S(2)}) collective-permute-start(bf16[2880,128]{1,0:T(8,128)(2,1)} %get-tuple-element.24.refs_3_.refs_4_.refs_0_), channel_id=1, source_target_pairs={{0,8},{64,72},{8,0},{72,64},{1,9},{65,73},{9,1},{73,65},{2,10},{66... | collective-permute-start | bytes 2211848 | tf_op jit(solution)/shard_map/ppermute | solution.py:40
  97.4 20.5 %copy-start.25 = (s32[4]{0:T(128)S(1)}, s32[4]{0:T(128)}, u32[]{:S(2)}) copy-start(s32[4]{0:T(128)} %get-tuple-element.57) | copy-start | bytes 52
  97.4 20.5 %copy-start.26 = (s32[4]{0:T(128)S(1)}, s32[4]{0:T(128)}, u32[]{:S(2)}) copy-start(s32[4]{0:T(128)} %get-tuple-element.58) | copy-start | bytes 52
  97.4 21.1 %copy-start.22 = (s32[4]{0:T(128)S(1)}, s32[4]{0:T(128)}, u32[]{:S(2)}) copy-start(s32[4]{0:T(128)} %copy-done.21) | copy-start | bytes 52
  97.4 21.2 %copy-start.23 = (s32[4]{0:T(128)S(1)}, s32[4]{0:T(128)}, u32[]{:S(2)}) copy-start(s32[4]{0:T(128)} %get-tuple-element.42) | copy-start | bytes 52
  113.4 20.8 %collective-permute-start.14 = (bf16[208,640]{1,0:T(8,128)(2,1)}, bf16[208,640]{1,0:T(8,128)(2,1)S(1)}, u32[]{:S(2)}, u32[]{:S(2)}) collective-permute-start(bf16[208,640]{1,0:T(8,128)(2,1)} %get-tuple-element.27), channel_id=1, source_target_pairs={{0,48},{16,0},{32,16},{48,32},{1,49},{17,1},{33,17},{49,33},{2,50}... | collective-permute-start | bytes 798728 | tf_op jit(solution)/shard_map/ppermute | solution.py:36
  113.4 25.9 %collective-permute-start.15 = (bf16[208,640]{1,0:T(8,128)(2,1)}, bf16[208,640]{1,0:T(8,128)(2,1)S(1)}, u32[]{:S(2)}, u32[]{:S(2)}) collective-permute-start(bf16[208,640]{1,0:T(8,128)(2,1)} %get-tuple-element.28), channel_id=1, source_target_pairs={{0,16},{16,32},{32,48},{48,0},{1,17},{17,33},{33,49},{49,1},{2,18}... | collective-permute-start | bytes 798728 | tf_op jit(solution)/shard_map/ppermute | solution.py:36
  115.4 23.9 %collective-permute-start.16 = (bf16[208,640]{1,0:T(8,128)(2,1)}, bf16[208,640]{1,0:T(8,128)(2,1)S(1)}, u32[]{:S(2)}, u32[]{:S(2)}) collective-permute-start(bf16[208,640]{1,0:T(8,128)(2,1)} %get-tuple-element.29), channel_id=1, source_target_pairs={{0,32},{16,48},{32,0},{48,16},{1,33},{17,49},{33,1},{49,17},{2,34}... | collective-permute-start | bytes 798728 | tf_op jit(solution)/shard_map/ppermute | solution.py:36
  134.2 6.7 %copy-start.15 = (bf16[208,640]{1,0:T(8,128)(2,1)}, bf16[208,640]{1,0:T(8,128)(2,1)S(1)}, u32[]{:S(2)}) copy-start(bf16[208,640]{1,0:T(8,128)(2,1)S(1)} %collective-permute-done.14.a1) | copy-start | bytes 798724
  134.2 14.1 %collective-permute-start.17 = (bf16[208,640]{1,0:T(8,128)(2,1)}, bf16[208,640]{1,0:T(8,128)(2,1)}, u32[]{:S(2)}, u32[]{:S(2)}) collective-permute-start(bf16[208,640]{1,0:T(8,128)(2,1)} %get-tuple-element.31), channel_id=1, source_target_pairs={{0,72},{64,0},{8,64},{72,8},{1,73},{65,1},{9,65},{73,9},{2,74},{66... | collective-permute-start | bytes 798728 | tf_op jit(solution)/shard_map/ppermute | solution.py:40
  139.3 1.6 copy-start.16
  139.3 11.3 %collective-permute-start.18 = (bf16[208,640]{1,0:T(8,128)(2,1)}, bf16[208,640]{1,0:T(8,128)(2,1)}, u32[]{:S(2)}, u32[]{:S(2)}) collective-permute-start(bf16[208,640]{1,0:T(8,128)(2,1)} %get-tuple-element.33), channel_id=1, source_target_pairs={{0,64},{64,8},{8,72},{72,0},{1,65},{65,9},{9,73},{73,1},{2,66},{66... | collective-permute-start | bytes 798728 | tf_op jit(solution)/shard_map/ppermute | solution.py:40
  139.3 1.6 copy-start.17
  139.3 11.3 %collective-permute-start.19 = (bf16[208,640]{1,0:T(8,128)(2,1)}, bf16[208,640]{1,0:T(8,128)(2,1)}, u32[]{:S(2)}, u32[]{:S(2)}) collective-permute-start(bf16[208,640]{1,0:T(8,128)(2,1)} %get-tuple-element.34), channel_id=1, source_target_pairs={{0,8},{64,72},{8,0},{72,64},{1,9},{65,73},{9,1},{73,65},{2,10},{66... | collective-permute-start | bytes 798728 | tf_op jit(solution)/shard_map/ppermute | solution.py:40
  140.8 23.2 %collective-permute-start.24 = (bf16[384,3072]{1,0:T(8,128)(2,1)}, bf16[384,3072]{1,0:T(8,128)(2,1)}, u32[]{:S(2)}, u32[]{:S(2)}) collective-permute-start(bf16[384,3072]{1,0:T(8,128)(2,1)} %collective-permute-done.23.refs_2_), channel_id=1, source_target_pairs={{0,1},{1,0},{2,3},{3,2},{4,5},{5,4},{6,7},{7,6},{8,9},{9,8},{10,11... | collective-permute-start | bytes 7077896 | tf_op jit(solution)/shard_map/ppermute | solution.py:44
  140.9 23.1 %collective-permute-start.26 = (bf16[384,3072]{1,0:T(8,128)(2,1)}, bf16[384,3072]{1,0:T(8,128)(2,1)S(1)}, u32[]{:S(2)}, u32[]{:S(2)}) collective-permute-start(bf16[384,3072]{1,0:T(8,128)(2,1)} %collective-permute-done.25.refs_4_), channel_id=1, source_target_pairs={{0,1},{1,0},{2,3},{3,2},{4,5},{5,4},{6,7},{7,6},{8,9},{9,8},{10,11... | collective-permute-start | bytes 7077896 | tf_op jit(solution)/shard_map/ppermute | solution.py:44
  154.0 1.7 collective-permute-start.20
  155.7 3.4 %copy-start.7 = (bf16[320,384]{1,0:T(8,128)(2,1)}, bf16[320,384]{1,0:T(8,128)(2,1)S(1)}, u32[]{:S(2)}) copy-start(bf16[320,384]{1,0:T(8,128)(2,1)S(1)} %collective-permute-done.20.theirs) | copy-start | bytes 737284
  155.8 8.2 %collective-permute-start.21 = (bf16[160,384]{1,0:T(8,128)(2,1)S(1)}, bf16[160,384]{1,0:T(8,128)(2,1)S(1)}, u32[]{:S(2)}, u32[]{:S(2)}) collective-permute-start(bf16[160,384]{1,0:T(8,128)(2,1)S(1)} %pad_maximum_fusion.1), channel_id=1, source_target_pairs={{0,2},{2,4},{4,6},{6,0},{1,3},{3,5},{5,7},{7,1},{8,10},{10,12},{12... | collective-permute-start | bytes 368648 | tf_op jit(solution)/shard_map/ppermute | solution.py:32
  155.9 8.1 %collective-permute-start.22 = (bf16[160,384]{1,0:T(8,128)(2,1)S(1)}, bf16[160,384]{1,0:T(8,128)(2,1)S(1)}, u32[]{:S(2)}, u32[]{:S(2)}) collective-permute-start(bf16[160,384]{1,0:T(8,128)(2,1)S(1)} %pad_maximum_fusion.2), channel_id=1, source_target_pairs={{0,6},{2,0},{4,2},{6,4},{1,7},{3,1},{5,3},{7,5},{8,14},{10,8},{12,... | collective-permute-start | bytes 368648 | tf_op jit(solution)/shard_map/ppermute | solution.py:32
  164.0 14.4 %collective-permute-start.27 = (bf16[80,3072]{1,0:T(8,128)(2,1)}, bf16[80,3072]{1,0:T(8,128)(2,1)S(1)}, u32[]{:S(2)}, u32[]{:S(2)}) collective-permute-start(bf16[80,3072]{1,0:T(8,128)(2,1)} %far_output.1), channel_id=1, source_target_pairs={{0,4},{2,6},{4,0},{6,2},{1,5},{3,7},{5,1},{7,3},{8,12},{10,14},{12... | collective-permute-start | bytes 1474568 | tf_op jit(solution)/shard_map/ppermute | solution.py:32
  164.0 0.7 copy-start.18
  164.0 0.7 copy-start.19
  164.7 1.4 copy-start.6

commit v2 on v0

--- a/solution.py
+++ b/solution.py
@@ -310,11 +310,13 @@
 
         @pl.when(mixed)
         def _():
-            def one(step, inner):
-                heads(i, low + step, 1, True)
+            size = 2 if last and not carried and n_q == 3 else 1
+
+            def some(step, inner):
+                heads(i, low + size * step, size, True)
                 return inner
 
-            lax.fori_loop(0, count, one, 0)
+            lax.fori_loop(0, count // size, some, 0)
 
         @pl.when(jnp.logical_not(mixed))
         def _():

time: 180 us -> 181 us (level); the launches traced: 176 us -> 180 us
  Pallas kernels: 76 us -> 86.4 us
  waiting for transfers between devices: 34.6 us -> 29.7 us
    pallas_call x4, Pallas kernels: 42.1 us -> 52.5 us  [attend(): pl.pallas_call(functools.partial(attend_kernel, places=places, n_k=n_k, c...]
    ppermute x6, waiting for transfers between devices: 6.44 us -> 2.88 us  [shift_y(): lax.ppermute(value, Y_AXES, [(Y_INDEX[i], Y_INDEX[(i + step) % 4]) for i...]
    ppermute x6, starting transfers between devices: 11.5 us -> 9.33 us  [shift_z(): return lax.ppermute(value, 'z', [(i, (i + step) % 4) for i in range(4)])]
  transfers between devices with their start and end apart: 30 -> 30, of which waited for: 12 -> 10; matrix products, arithmetic and copies ran while one was open for 8% -> 8% of each run, Pallas kernels for 43% -> 48%
where the time goes in v2:
time: 181 us; the launch traced here: 180 us
  Pallas kernels  86.4 us (48%)
  starting transfers between devices  42.7 us (24%)
  waiting for transfers between devices  29.7 us (16%)
  other arithmetic  13 us (7%)
  local copies, waits for them, and re-layouts  7.25 us (4%)
    pallas_call x4, Pallas kernels, attend(): pl.pallas_call(functools.partial(attend_kernel, places=places, n_k=n_k, c...  52.5 us
    pallas_call x1, Pallas kernels, project(): pl.pallas_call(project_kernel, out_shape=[jax.ShapeDtypeStruct((2880, 128...  17.8 us
    ppermute x6, waiting for transfers between devices, shift_z(): return lax.ppermute(value, 'z', [(i, (i + step) % 4) for i in range(4)])  12.8 us
    ppermute x8, starting transfers between devices, shift_x(): return lax.ppermute(value, 'x', [(i, (i + step) % 4) for i in range(4)])  11.8 us
    ppermute x6, starting transfers between devices, shift_z(): return lax.ppermute(value, 'z', [(i, (i + step) % 4) for i in range(4)])  9.33 us
    ppermute x6, starting transfers between devices, shift_y(): lax.ppermute(value, Y_AXES, [(Y_INDEX[i], Y_INDEX[(i + step) % 4]) for i...  8.2 us
    all_to_all x1, starting transfers between devices, local(): lax.all_to_all(jnp.broadcast_to(packed[None], (16, 3, 128)), tiles_axes,...  8.05 us
    pallas_call x1, Pallas kernels, near_output(): pl.pallas_call(near_output_kernel, out_shape=jax.ShapeDtypeStruct((OWN, D...  7.95 us
  transfers between devices with their start and end apart: 30, of which 10 were waited for; matrix products, arithmetic and copies ran while one was open for 8% of the time, Pallas kernels for 48%

profile of v2, /device:TPU:0, one launch (start us, length us, event | category | flops | bytes accessed | tf_op | source)
XLA Modules:
  0.0 180.4 jit_solution(8489043790620189217)
XLA Ops:
  0.0 1.6 collective-permute-start.1
  1.6 1.7 collective-permute-start.2
  3.2 1.9 %collective-permute-start.3 = (bf16[80,3072]{1,0:T(8,128)(2,1)}, bf16[80,3072]{1,0:T(8,128)(2,1)S(1)}, u32[]{:S(2)}, u32[]{:S(2)}) collective-permute-start(bf16[80,3072]{1,0:T(8,128)(2,1)} %c0.1), channel_id=1, source_target_pairs={{0,4},{2,6},{4,0},{6,2},{1,5},{3,7},{5,1},{7,3},{8,12},{10,14},{12... | collective-permute-start | bytes 1474568 | tf_op jit(solution)/shard_map/ppermute | solution.py:32
  5.1 0.5 collective-permute-start
  5.7 0.7 convert_element_type.17
  6.3 0.1 multiply_cosine_fusion
  6.5 0.1 fusion.19
  6.7 0.6 broadcast_in_dim.120
  7.3 8.0 %all-to-all-start = ((f32[16,3,128]{2,1,0:T(4,128)}), f32[16,3,128]{2,1,0:T(4,128)S(1)}, u32[]{:S(2)}, u32[]{:S(2)}) async-start(f32[16,3,128]{2,1,0:T(4,128)} %broadcast_in_dim.120), calls=%async_computation | async-start | bytes 65536 | tf_op jit(solution)/shard_map/all_to_all | solution.py:521
  15.5 1.2 subtract_multiply_fusion.1
  16.8 0.8 select_reduce_fusion
  18.9 3.0 %negate_select_fusion = (f32[640,128]{1,0:T(8,128)}, f32[640,128]{1,0:T(8,128)}) fusion(s32[128]{0:T(128)S(1)} %get-tuple-element.65, s32[128]{0:T(128)S(1)} %get-tuple-element.67, pred[640]{0:T(1024)(128)(4,1)S(1)} %fusion.13, pred[128]{0:T(512)(128)(4,1)S(1)} %get-tuple-element.63, f32[128]{0:T(128)S(1)} %mul.106, s32[640]{0:T(1024)S(1)} %fusion.15, ...), kind=kLoop, calls=%fused_computation.5 | loop fusion | flops 3031040 | bytes 676096 | tf_op jit(solution)/shard_map/jit(_where)/select_n | solution.py:76
  21.8 1.3 all-to-all-done
  23.1 0.7 broadcast_in_dim.121
  23.8 3.4 %all-to-all-start.1 = ((f32[8,16,3,128]{3,1,2,0:T(8,128)}), f32[8,16,3,128]{3,1,2,0:T(8,128)S(1)}, u32[]{:S(2)}, u32[]{:S(2)}) async-start(f32[8,16,3,128]{3,1,2,0:T(8,128)} %broadcast_in_dim.121), calls=%async_computation.1 | async-start | bytes 393216 | tf_op jit(solution)/shard_map/all_to_all | solution.py:524
  27.2 0.7 pad_add_fusion.2.info
  27.9 6.1 %all-to-all-done.1 = f32[8,16,3,128]{3,1,2,0:T(8,128)S(1)} async-done(((f32[8,16,3,128]{3,1,2,0:T(8,128)}), f32[8,16,3,128]{3,1,2,0:T(8,128)S(1)}, u32[]{:S(2)}, u32[]{:S(2)}) %all-to-all-start.1) | async-done | bytes 196640 | tf_op jit(solution)/shard_map/all_to_all | solution.py:524
  34.1 0.2 stack_reshape.6
  34.3 0.2 stack_reshape.7
  34.6 0.5 collective-permute-start.6
  35.1 0.3 collective-permute-start.7
  35.4 0.8 pad_maximum_fusion.mods
  36.2 0.3 collective-permute-done.5.c5
  36.5 0.7 collective-permute-done.6.c6
  37.2 0.7 collective-permute-done.7.c7
  37.9 0.1 copy-done.13
  38.0 0.7 copy-done.14
  38.7 17.8 %project.1 = (bf16[2880,128]{1,0:T(8,128)(2,1)}, bf16[2880,128]{1,0:T(8,128)(2,1)}) custom-call(s32[10]{0:T(128)} %pad_add_fusion.2.info, bf16[80,3072]{1,0:T(8,128)(2,1)} %c0.1, bf16[80,3072]{1,0:T(8,128)(2,1)} %copy-done.8, bf16[80,3072]{1,0:T(8,128)(2,1)} %copy-done.9, bf16[80,3072]{1,0:T(8,128)(2,1)} %copy-done.10, bf16[80,3072]{1,0:T(8,128)(2,1)} %copy-done.11, ...), custom_call_target="tpu_custom_call" | custom-call | tf_op jit(solution)/shard_map/project/pallas_call | solution.py:180
  56.4 0.7 collective-permute-start.8
  57.1 2.6 %collective-permute-start.9 = (bf16[2880,128]{1,0:T(8,128)(2,1)}, bf16[2880,128]{1,0:T(8,128)(2,1)S(1)}, u32[]{:S(2)}, u32[]{:S(2)}) collective-permute-start(bf16[2880,128]{1,0:T(8,128)(2,1)} %get-tuple-element.21.refs_0_.refs_3_.refs_1_), channel_id=1, source_target_pairs={{0,48},{16,0},{32,16},{48,32},{1,49},{17,1},{33,17},{49,33},{2,50}... | collective-permute-start | bytes 2211848 | tf_op jit(solution)/shard_map/ppermute | solution.py:36
  59.7 0.7 collective-permute-start.10
  60.4 2.6 %collective-permute-start.11 = (bf16[2880,128]{1,0:T(8,128)(2,1)}, bf16[2880,128]{1,0:T(8,128)(2,1)S(1)}, u32[]{:S(2)}, u32[]{:S(2)}) collective-permute-start(bf16[2880,128]{1,0:T(8,128)(2,1)} %get-tuple-element.22.refs_3_.refs_4_.refs_0_), channel_id=1, source_target_pairs={{0,72},{64,0},{8,64},{72,8},{1,73},{65,1},{9,65},{73,9},{2,74},{66... | collective-permute-start | bytes 2211848 | tf_op jit(solution)/shard_map/ppermute | solution.py:40
  63.0 0.7 subtract_clamp_fusion.limits
  63.6 12.8 %collective-permute-done.8.refs_1_.refs_4_.refs_2_ = bf16[2880,128]{1,0:T(8,128)(2,1)S(1)} collective-permute-done((bf16[2880,128]{1,0:T(8,128)(2,1)}, bf16[2880,128]{1,0:T(8,128)(2,1)S(1)}, u32[]{:S(2)}, u32[]{:S(2)}) %collective-permute-start.8) | collective-permute-done | bytes 737312 | tf_op jit(solution)/shard_map/ppermute | solution.py:36
  76.4 2.7 %collective-permute-done.10.refs_4_.refs_5_.refs_0_ = bf16[2880,128]{1,0:T(8,128)(2,1)S(1)} collective-permute-done((bf16[2880,128]{1,0:T(8,128)(2,1)}, bf16[2880,128]{1,0:T(8,128)(2,1)S(1)}, u32[]{:S(2)}, u32[]{:S(2)}) %collective-permute-start.10) | collective-permute-done | bytes 737312 | tf_op jit(solution)/shard_map/ppermute | solution.py:40
  79.1 0.6 collective-permute-start.23
  79.8 2.7 %collective-permute-start.25 = (bf16[384,3072]{1,0:T(8,128)(2,1)S(1)}, bf16[384,3072]{1,0:T(8,128)(2,1)}, u32[]{:S(2)}, u32[]{:S(2)}) collective-permute-start(bf16[384,3072]{1,0:T(8,128)(2,1)S(1)} %copy-done.3), channel_id=1, source_target_pairs={{0,6},{2,0},{4,2},{6,4},{1,7},{3,1},{5,3},{7,5},{8,14},{10,8},{12,... | collective-permute-start | bytes 7077896 | tf_op jit(solution)/shard_map/ppermute | solution.py:32
  82.5 0.9 collective-permute-start.12
  83.4 2.6 %collective-permute-start.13 = (bf16[2880,128]{1,0:T(8,128)(2,1)}, bf16[2880,128]{1,0:T(8,128)(2,1)}, u32[]{:S(2)}, u32[]{:S(2)}) collective-permute-start(bf16[2880,128]{1,0:T(8,128)(2,1)} %get-tuple-element.22.refs_3_.refs_4_.refs_0_), channel_id=1, source_target_pairs={{0,8},{64,72},{8,0},{72,64},{1,9},{65,73},{9,1},{73,65},{2,10},{66... | collective-permute-start | bytes 2211848 | tf_op jit(solution)/shard_map/ppermute | solution.py:40
  86.0 0.6 fusion.46
  86.7 14.5 %near_a.1.refs_8_ = f32[3,3,80,640]{3,2,1,0:T(8,128)} custom-call(s32[8]{0:T(128)} %copy-done.20, bf16[2880,128]{1,0:T(8,128)(2,1)} %get-tuple-element.21.refs_0_.refs_3_.refs_1_, bf16[2880,128]{1,0:T(8,128)(2,1)} %copy-done.1, bf16[2880,128]{1,0:T(8,128)(2,1)} %copy-done.2, bf16[2880,128]{1,0:T(8,128)(2,1)} %get-tuple-element.22.refs_3_.refs_4_.refs_0_, ...), custom_call_target="tpu_custom_call" | custom-call | flops 1000 | bytes 1000 | tf_op jit(solution)/shard_map/near_a/pallas_call | solution.py:377
  101.2 0.2 collective-permute-done.13.refs_7_.refs_2_
  101.4 12.6 %far_a.1 = (f32[3,80,640]{2,1,0:T(8,128)}, bf16[208,640]{1,0:T(8,128)(2,1)}, bf16[208,640]{1,0:T(8,128)(2,1)}, bf16[208,640]{1,0:T(8,128)(2,1)}) custom-call(s32[8]{0:T(128)} %copy-done.20, bf16[2880,128]{1,0:T(8,128)(2,1)} %get-tuple-element.21.refs_0_.refs_3_.refs_1_, bf16[2880,128]{1,0:T(8,128)(2,1)} %copy-done.1, bf16[2880,128]{1,0:T(8,128)(2,1)} %copy-done.2, ...), custom_call_target="tpu_custom_call" | custom-call | flops 1000 | bytes 1000 | tf_op jit(solution)/shard_map/far_a/pallas_call | solution.py:377
  114.1 2.0 %collective-permute-start.15 = (bf16[208,640]{1,0:T(8,128)(2,1)}, bf16[208,640]{1,0:T(8,128)(2,1)S(1)}, u32[]{:S(2)}, u32[]{:S(2)}) collective-permute-start(bf16[208,640]{1,0:T(8,128)(2,1)} %get-tuple-element.26), channel_id=1, source_target_pairs={{0,16},{16,32},{32,48},{48,0},{1,17},{17,33},{33,49},{49,1},{2,18}... | collective-permute-start | bytes 798728 | tf_op jit(solution)/shard_map/ppermute | solution.py:36
  116.1 3.1 %collective-permute-start.16 = (bf16[208,640]{1,0:T(8,128)(2,1)}, bf16[208,640]{1,0:T(8,128)(2,1)S(1)}, u32[]{:S(2)}, u32[]{:S(2)}) collective-permute-start(bf16[208,640]{1,0:T(8,128)(2,1)} %get-tuple-element.27), channel_id=1, source_target_pairs={{0,32},{16,48},{32,0},{48,16},{1,33},{17,49},{33,1},{49,17},{2,34}... | collective-permute-start | bytes 798728 | tf_op jit(solution)/shard_map/ppermute | solution.py:36
  119.1 0.7 pad_add_fusion.3.limits
  119.8 0.5 add_multiply_fusion
  120.3 15.6 %rest_b.1 = (bf16[208,640]{1,0:T(8,128)(2,1)}, bf16[208,640]{1,0:T(8,128)(2,1)}, bf16[208,640]{1,0:T(8,128)(2,1)}) custom-call(s32[8]{0:T(128)} %pad_add_fusion.3.limits, bf16[2880,128]{1,0:T(8,128)(2,1)} %copy-done.4, bf16[2880,128]{1,0:T(8,128)(2,1)} %copy-done.5, bf16[2880,128]{1,0:T(8,128)(2,1)} %collective-permute-done.13.refs_7_.refs_2_, ...), custom_call_target="tpu_custom_call" | custom-call | flops 1000 | bytes 1000 | tf_op jit(solution)/shard_map/rest_b/pallas_call | solution.py:377
  135.9 0.3 collective-permute-start.17
  136.3 2.0 %collective-permute-start.18 = (bf16[208,640]{1,0:T(8,128)(2,1)}, bf16[208,640]{1,0:T(8,128)(2,1)}, u32[]{:S(2)}, u32[]{:S(2)}) collective-permute-start(bf16[208,640]{1,0:T(8,128)(2,1)} %get-tuple-element.31), channel_id=1, source_target_pairs={{0,64},{64,8},{8,72},{72,0},{1,65},{65,9},{9,73},{73,1},{2,66},{66... | collective-permute-start | bytes 798728 | tf_op jit(solution)/shard_map/ppermute | solution.py:40
  138.4 0.6 copy-done.17
  139.0 1.2 pad_add_fusion.1.order
  140.2 9.8 %own_b.1 = f32[3,80,640]{2,1,0:T(8,128)} custom-call(s32[8]{0:T(128)} %pad_add_fusion.3.limits, bf16[2880,128]{1,0:T(8,128)(2,1)} %get-tuple-element.22.refs_3_.refs_4_.refs_0_, bf16[2880,128]{1,0:T(8,128)(2,1)} %get-tuple-element.21.refs_0_.refs_3_.refs_1_, bf16[2880,128]{1,0:T(8,128)(2,1)} %copy-done.1, bf16[2880,128]{1,0:T(8,128)(2,1)} %copy-done.2, ...), custom_call_target="tpu_custom_call" | custom-call | flops 1000 | bytes 1000 | tf_op jit(solution)/shard_map/own_b/pallas_call | solution.py:377
  150.0 3.4 %merge.1 = (bf16[320,384]{1,0:T(8,128)(2,1)}, bf16[320,384]{1,0:T(8,128)(2,1)}) custom-call(s32[8]{0:T(128)} %pad_add_fusion.1.order, f32[3,80,640]{2,1,0:T(8,128)} %get-tuple-element.24.own_a, bf16[208,640]{1,0:T(8,128)(2,1)} %copy-done.15, bf16[208,640]{1,0:T(8,128)(2,1)} %copy-done.16, bf16[208,640]{1,0:T(8,128)(2,1)} %copy-done.17, f32[3,80,640]{2,1,0:T(8,128)} %own_b.1, ...), custom_call_target="tpu_custom_call" | custom-call | tf_op jit(solution)/shard_map/merge/pallas_call | solution.py:423
  153.4 0.5 collective-permute-start.20
  153.9 0.9 fusion.41
  154.8 0.5 collective-permute-done.20.theirs
  155.4 3.3 %collective-permute-start.22 = (bf16[160,384]{1,0:T(8,128)(2,1)S(1)}, bf16[160,384]{1,0:T(8,128)(2,1)S(1)}, u32[]{:S(2)}, u32[]{:S(2)}) collective-permute-start(bf16[160,384]{1,0:T(8,128)(2,1)S(1)} %pad_maximum_fusion.2), channel_id=1, source_target_pairs={{0,6},{2,0},{4,2},{6,4},{1,7},{3,1},{5,3},{7,5},{8,14},{10,8},{12,... | collective-permute-start | bytes 368648 | tf_op jit(solution)/shard_map/ppermute | solution.py:32
  158.7 4.8 %far_output.1 = bf16[80,3072]{1,0:T(8,128)(2,1)} custom-call(bf16[320,384]{1,0:T(8,128)(2,1)} %get-tuple-element.33.mine, bf16[320,384]{1,0:T(8,128)(2,1)} %copy-done.7, bf16[384,3072]{1,0:T(8,128)(2,1)} %w_here.1, bf16[384,3072]{1,0:T(8,128)(2,1)} %collective-permute-done.refs_1_.w_other), custom_call_target="tpu_custom_call" | custom-call | flops 1000 | bytes 1000 | tf_op jit(solution)/shard_map/far_output/pallas_call | solution.py:449
  163.6 0.6 copy-done.18
  164.3 1.4 copy-done.6
  165.7 7.9 %near_output.1 = f32[80,3072]{1,0:T(8,128)} custom-call(bf16[320,384]{1,0:T(8,128)(2,1)} %get-tuple-element.33.mine, bf16[320,384]{1,0:T(8,128)(2,1)} %copy-done.7, bf16[160,384]{1,0:T(8,128)(2,1)} %copy-done.18, bf16[160,384]{1,0:T(8,128)(2,1)} %copy-done.19, bf16[384,3072]{1,0:T(8,128)(2,1)} %w_here.1, ...), custom_call_target="tpu_custom_call" | custom-call | tf_op jit(solution)/shard_map/near_output/pallas_call | solution.py:479
  173.6 4.5 %collective-permute-done.27 = bf16[80,3072]{1,0:T(8,128)(2,1)S(1)} collective-permute-done((bf16[80,3072]{1,0:T(8,128)(2,1)}, bf16[80,3072]{1,0:T(8,128)(2,1)S(1)}, u32[]{:S(2)}, u32[]{:S(2)}) %collective-permute-start.27) | collective-permute-done | bytes 491552 | tf_op jit(solution)/shard_map/ppermute | solution.py:32
  178.2 2.3 %multiply_convert_fusion = bf16[80,3072]{1,0:T(8,128)(2,1)} fusion(f32[80,3072]{1,0:T(8,128)} %near_output.1, bf16[80,3072]{1,0:T(8,128)(2,1)S(1)} %collective-permute-done.27, f32[3072]{0:T(1024)S(1)} %bitcast.22, f32[3072]{0:T(1024)S(1)} %bitcast.24, f32[3072]{0:T(1024)S(1)} %bitcast.21, f32[3072]{0:T(1024)S(1)} %bitcast.23, pred[80]{0:T(512)(128)(4,1)S(1)} %fusion.36, ...), kind=kLoop, calls=%fused_computation | loop fusion | flops 1720320 | bytes 2015392 | tf_op jit(solution)/shard_map/convert_element_type | solution.py:590
  (112 shorter events, 1.4 us)
Async XLA Ops:
  0.0 6.4 %copy-start = (bf16[512,144]{0,1:T(8,128)(2,1)S(1)}, bf16[512,144]{0,1:T(8,128)(2,1)}, u32[]{:S(2)}) copy-start(bf16[512,144]{0,1:T(8,128)(2,1)} %param.17) | copy-start | bytes 442372
  0.0 34.5 %collective-permute-start.1 = (bf16[80,3072]{1,0:T(8,128)(2,1)}, bf16[80,3072]{1,0:T(8,128)(2,1)S(1)}, u32[]{:S(2)}, u32[]{:S(2)}) collective-permute-start(bf16[80,3072]{1,0:T(8,128)(2,1)} %c0.1), channel_id=1, source_target_pairs={{0,2},{2,4},{4,6},{6,0},{1,3},{3,5},{5,7},{7,1},{8,10},{10,12},{12... | collective-permute-start | bytes 1474568 | tf_op jit(solution)/shard_map/ppermute | solution.py:32
  1.6 33.0 %collective-permute-start.2 = (bf16[80,3072]{1,0:T(8,128)(2,1)}, bf16[80,3072]{1,0:T(8,128)(2,1)S(1)}, u32[]{:S(2)}, u32[]{:S(2)}) collective-permute-start(bf16[80,3072]{1,0:T(8,128)(2,1)} %c0.1), channel_id=1, source_target_pairs={{0,6},{2,0},{4,2},{6,4},{1,7},{3,1},{5,3},{7,5},{8,14},{10,8},{12,... | collective-permute-start | bytes 1474568 | tf_op jit(solution)/shard_map/ppermute | solution.py:32
  3.2 31.9 %collective-permute-start.3 = (bf16[80,3072]{1,0:T(8,128)(2,1)}, bf16[80,3072]{1,0:T(8,128)(2,1)S(1)}, u32[]{:S(2)}, u32[]{:S(2)}) collective-permute-start(bf16[80,3072]{1,0:T(8,128)(2,1)} %c0.1), channel_id=1, source_target_pairs={{0,4},{2,6},{4,0},{6,2},{1,5},{3,7},{5,1},{7,3},{8,12},{10,14},{12... | collective-permute-start | bytes 1474568 | tf_op jit(solution)/shard_map/ppermute | solution.py:32
  5.1 31.0 %collective-permute-start.4 = (bf16[80,3072]{1,0:T(8,128)(2,1)}, bf16[80,3072]{1,0:T(8,128)(2,1)S(1)}, u32[]{:S(2)}, u32[]{:S(2)}) collective-permute-start(bf16[80,3072]{1,0:T(8,128)(2,1)} %c0.1), channel_id=1, source_target_pairs={{0,1},{1,0},{2,3},{3,2},{4,5},{5,4},{6,7},{7,6},{8,9},{9,8},{10,11... | collective-permute-start | bytes 1474568 | tf_op jit(solution)/shard_map/ppermute | solution.py:44
  5.1 74.0 %collective-permute-start = (bf16[384,3072]{1,0:T(8,128)(2,1)}, bf16[384,3072]{1,0:T(8,128)(2,1)}, u32[]{:S(2)}, u32[]{:S(2)}) collective-permute-start(bf16[384,3072]{1,0:T(8,128)(2,1)} %w_here.1), channel_id=1, source_target_pairs={{0,1},{1,0},{2,3},{3,2},{4,5},{5,4},{6,7},{7,6},{8,9},{9,8},{10,11... | collective-permute-start | bytes 7077896 | tf_op jit(solution)/shard_map/ppermute | solution.py:44
  7.3 15.8 %all-to-all-start = ((f32[16,3,128]{2,1,0:T(4,128)}), f32[16,3,128]{2,1,0:T(4,128)S(1)}, u32[]{:S(2)}, u32[]{:S(2)}) async-start(f32[16,3,128]{2,1,0:T(4,128)} %broadcast_in_dim.120), calls=%async_computation | async-start | bytes 65536 | tf_op jit(solution)/shard_map/all_to_all | solution.py:521
  16.7 17.3 %copy-start.21 = (s32[4]{0:T(128)}, s32[4]{0:T(128)S(1)}, u32[]{:S(2)}) copy-start(s32[4]{0:T(128)S(1)} %get-tuple-element.61) | copy-start | bytes 52
  17.6 16.4 %copy-start.24 = (s32[8]{0:T(128)}, s32[8]{0:T(128)S(1)}, u32[]{:S(2)}) copy-start(s32[8]{0:T(128)S(1)} %select_reduce_fusion) | copy-start | bytes 100
  23.8 10.2 %all-to-all-start.1 = ((f32[8,16,3,128]{3,1,2,0:T(8,128)}), f32[8,16,3,128]{3,1,2,0:T(8,128)S(1)}, u32[]{:S(2)}, u32[]{:S(2)}) async-start(f32[8,16,3,128]{3,1,2,0:T(8,128)} %broadcast_in_dim.121), calls=%async_computation.1 | async-start | bytes 393216 | tf_op jit(solution)/shard_map/all_to_all | solution.py:524
  34.5 4.2 %copy-start.8 = (bf16[80,3072]{1,0:T(8,128)(2,1)}, bf16[80,3072]{1,0:T(8,128)(2,1)S(1)}, u32[]{:S(2)}) copy-start(bf16[80,3072]{1,0:T(8,128)(2,1)S(1)} %collective-permute-done.1.c1) | copy-start | bytes 1474564
  34.5 1.9 %collective-permute-start.5 = (bf16[80,3072]{1,0:T(8,128)(2,1)S(1)}, bf16[80,3072]{1,0:T(8,128)(2,1)S(1)}, u32[]{:S(2)}, u32[]{:S(2)}) collective-permute-start(bf16[80,3072]{1,0:T(8,128)(2,1)S(1)} %collective-permute-done.1.c1), channel_id=1, source_target_pairs={{0,1},{1,0},{2,3},{3,2},{4,5},{5,4},{6,7},{7,6},{8,9},{9,8},{10,11... | collective-permute-start | bytes 1474568 | tf_op jit(solution)/shard_map/ppermute | solution.py:44
  34.6 3.2 %copy-start.9 = (bf16[80,3072]{1,0:T(8,128)(2,1)}, bf16[80,3072]{1,0:T(8,128)(2,1)S(1)}, u32[]{:S(2)}) copy-start(bf16[80,3072]{1,0:T(8,128)(2,1)S(1)} %collective-permute-done.2.c2) | copy-start | bytes 1474564
  34.6 2.5 %collective-permute-start.6 = (bf16[80,3072]{1,0:T(8,128)(2,1)S(1)}, bf16[80,3072]{1,0:T(8,128)(2,1)S(1)}, u32[]{:S(2)}, u32[]{:S(2)}) collective-permute-start(bf16[80,3072]{1,0:T(8,128)(2,1)S(1)} %collective-permute-done.2.c2), channel_id=1, source_target_pairs={{0,1},{1,0},{2,3},{3,2},{4,5},{5,4},{6,7},{7,6},{8,9},{9,8},{10,11... | collective-permute-start | bytes 1474568 | tf_op jit(solution)/shard_map/ppermute | solution.py:44
  35.1 2.8 %copy-start.10 = (bf16[80,3072]{1,0:T(8,128)(2,1)}, bf16[80,3072]{1,0:T(8,128)(2,1)S(1)}, u32[]{:S(2)}) copy-start(bf16[80,3072]{1,0:T(8,128)(2,1)S(1)} %collective-permute-done.3.c3) | copy-start | bytes 1474564
  35.1 2.7 %collective-permute-start.7 = (bf16[80,3072]{1,0:T(8,128)(2,1)S(1)}, bf16[80,3072]{1,0:T(8,128)(2,1)S(1)}, u32[]{:S(2)}, u32[]{:S(2)}) collective-permute-start(bf16[80,3072]{1,0:T(8,128)(2,1)S(1)} %collective-permute-done.3.c3), channel_id=1, source_target_pairs={{0,1},{1,0},{2,3},{3,2},{4,5},{5,4},{6,7},{7,6},{8,9},{9,8},{10,11... | collective-permute-start | bytes 1474568 | tf_op jit(solution)/shard_map/ppermute | solution.py:44
  36.2 1.7 copy-start.11
  36.5 2.2 %copy-start.12 = (bf16[80,3072]{1,0:T(8,128)(2,1)}, bf16[80,3072]{1,0:T(8,128)(2,1)S(1)}, u32[]{:S(2)}) copy-start(bf16[80,3072]{1,0:T(8,128)(2,1)S(1)} %collective-permute-done.5.c5) | copy-start | bytes 1474564
  37.2 0.8 copy-start.13
  37.9 0.8 copy-start.14
  38.7 40.5 %copy-start.3 = (bf16[384,3072]{1,0:T(8,128)(2,1)S(1)}, bf16[384,3072]{1,0:T(8,128)(2,1)}, u32[]{:S(2)}) copy-start(bf16[384,3072]{1,0:T(8,128)(2,1)} %w_here.1) | copy-start | bytes 7077892
  56.4 20.0 %collective-permute-start.8 = (bf16[2880,128]{1,0:T(8,128)(2,1)}, bf16[2880,128]{1,0:T(8,128)(2,1)S(1)}, u32[]{:S(2)}, u32[]{:S(2)}) collective-permute-start(bf16[2880,128]{1,0:T(8,128)(2,1)} %get-tuple-element.21.refs_0_.refs_3_.refs_1_), channel_id=1, source_target_pairs={{0,16},{16,32},{32,48},{48,0},{1,17},{17,33},{33,49},{49,1},{2,18}... | collective-permute-start | bytes 2211848 | tf_op jit(solution)/shard_map/ppermute | solution.py:36
  57.1 19.3 %collective-permute-start.9 = (bf16[2880,128]{1,0:T(8,128)(2,1)}, bf16[2880,128]{1,0:T(8,128)(2,1)S(1)}, u32[]{:S(2)}, u32[]{:S(2)}) collective-permute-start(bf16[2880,128]{1,0:T(8,128)(2,1)} %get-tuple-element.21.refs_0_.refs_3_.refs_1_), channel_id=1, source_target_pairs={{0,48},{16,0},{32,16},{48,32},{1,49},{17,1},{33,17},{49,33},{2,50}... | collective-permute-start | bytes 2211848 | tf_op jit(solution)/shard_map/ppermute | solution.py:36
  59.7 19.4 %collective-permute-start.10 = (bf16[2880,128]{1,0:T(8,128)(2,1)}, bf16[2880,128]{1,0:T(8,128)(2,1)S(1)}, u32[]{:S(2)}, u32[]{:S(2)}) collective-permute-start(bf16[2880,128]{1,0:T(8,128)(2,1)} %get-tuple-element.22.refs_3_.refs_4_.refs_0_), channel_id=1, source_target_pairs={{0,64},{64,8},{8,72},{72,0},{1,65},{65,9},{9,73},{73,1},{2,66},{66... | collective-permute-start | bytes 2211848 | tf_op jit(solution)/shard_map/ppermute | solution.py:40
  60.4 18.7 %collective-permute-start.11 = (bf16[2880,128]{1,0:T(8,128)(2,1)}, bf16[2880,128]{1,0:T(8,128)(2,1)S(1)}, u32[]{:S(2)}, u32[]{:S(2)}) collective-permute-start(bf16[2880,128]{1,0:T(8,128)(2,1)} %get-tuple-element.22.refs_3_.refs_4_.refs_0_), channel_id=1, source_target_pairs={{0,72},{64,0},{8,64},{72,8},{1,73},{65,1},{9,65},{73,9},{2,74},{66... | collective-permute-start | bytes 2211848 | tf_op jit(solution)/shard_map/ppermute | solution.py:40
  63.6 22.4 %copy-start.20 = (s32[8]{0:T(128)}, s32[8]{0:T(128)S(1)}, u32[]{:S(2)}) copy-start(s32[8]{0:T(128)S(1)} %subtract_clamp_fusion.limits) | copy-start | bytes 100
  76.4 10.2 %copy-start.1 = (bf16[2880,128]{1,0:T(8,128)(2,1)}, bf16[2880,128]{1,0:T(8,128)(2,1)S(1)}, u32[]{:S(2)}) copy-start(bf16[2880,128]{1,0:T(8,128)(2,1)S(1)} %collective-permute-done.8.refs_1_.refs_4_.refs_2_) | copy-start | bytes 2211844
  76.4 10.2 %copy-start.2 = (bf16[2880,128]{1,0:T(8,128)(2,1)}, bf16[2880,128]{1,0:T(8,128)(2,1)S(1)}, u32[]{:S(2)}) copy-start(bf16[2880,128]{1,0:T(8,128)(2,1)S(1)} %collective-permute-done.9.refs_2_.refs_5_.refs_3_) | copy-start | bytes 2211844
  79.1 3.3 %copy-start.4 = (bf16[2880,128]{1,0:T(8,128)(2,1)}, bf16[2880,128]{1,0:T(8,128)(2,1)S(1)}, u32[]{:S(2)}) copy-start(bf16[2880,128]{1,0:T(8,128)(2,1)S(1)} %collective-permute-done.10.refs_4_.refs_5_.refs_0_) | copy-start | bytes 2211844
  79.1 4.3 %copy-start.5 = (bf16[2880,128]{1,0:T(8,128)(2,1)}, bf16[2880,128]{1,0:T(8,128)(2,1)S(1)}, u32[]{:S(2)}) copy-start(bf16[2880,128]{1,0:T(8,128)(2,1)S(1)} %collective-permute-done.11.refs_5_.refs_6_.refs_1_) | copy-start | bytes 2211844
  79.1 59.1 %collective-permute-start.23 = (bf16[384,3072]{1,0:T(8,128)(2,1)S(1)}, bf16[384,3072]{1,0:T(8,128)(2,1)}, u32[]{:S(2)}, u32[]{:S(2)}) collective-permute-start(bf16[384,3072]{1,0:T(8,128)(2,1)S(1)} %copy-done.3), channel_id=1, source_target_pairs={{0,2},{2,4},{4,6},{6,0},{1,3},{3,5},{5,7},{7,1},{8,10},{10,12},{12... | collective-permute-start | bytes 7077896 | tf_op jit(solution)/shard_map/ppermute | solution.py:32
  79.8 59.2 %collective-permute-start.25 = (bf16[384,3072]{1,0:T(8,128)(2,1)S(1)}, bf16[384,3072]{1,0:T(8,128)(2,1)}, u32[]{:S(2)}, u32[]{:S(2)}) collective-permute-start(bf16[384,3072]{1,0:T(8,128)(2,1)S(1)} %copy-done.3), channel_id=1, source_target_pairs={{0,6},{2,0},{4,2},{6,4},{1,7},{3,1},{5,3},{7,5},{8,14},{10,8},{12,... | collective-permute-start | bytes 7077896 | tf_op jit(solution)/shard_map/ppermute | solution.py:32
  82.5 18.8 %collective-permute-start.12 = (bf16[2880,128]{1,0:T(8,128)(2,1)}, bf16[2880,128]{1,0:T(8,128)(2,1)}, u32[]{:S(2)}, u32[]{:S(2)}) collective-permute-start(bf16[2880,128]{1,0:T(8,128)(2,1)} %get-tuple-element.21.refs_0_.refs_3_.refs_1_), channel_id=1, source_target_pairs={{0,32},{16,48},{32,0},{48,16},{1,33},{17,49},{33,1},{49,17},{2,34}... | collective-permute-start | bytes 2211848 | tf_op jit(solution)/shard_map/ppermute | solution.py:36
  83.4 18.0 %collective-permute-start.13 = (bf16[2880,128]{1,0:T(8,128)(2,1)}, bf16[2880,128]{1,0:T(8,128)(2,1)}, u32[]{:S(2)}, u32[]{:S(2)}) collective-permute-start(bf16[2880,128]{1,0:T(8,128)(2,1)} %get-tuple-element.22.refs_3_.refs_4_.refs_0_), channel_id=1, source_target_pairs={{0,8},{64,72},{8,0},{72,64},{1,9},{65,73},{9,1},{73,65},{2,10},{66... | collective-permute-start | bytes 2211848 | tf_op jit(solution)/shard_map/ppermute | solution.py:40
  101.2 17.9 %copy-start.25 = (s32[4]{0:T(128)S(1)}, s32[4]{0:T(128)}, u32[]{:S(2)}) copy-start(s32[4]{0:T(128)} %get-tuple-element.55) | copy-start | bytes 52
  101.2 17.9 %copy-start.26 = (s32[4]{0:T(128)S(1)}, s32[4]{0:T(128)}, u32[]{:S(2)}) copy-start(s32[4]{0:T(128)} %get-tuple-element.56) | copy-start | bytes 52
  101.2 18.6 %copy-start.22 = (s32[4]{0:T(128)S(1)}, s32[4]{0:T(128)}, u32[]{:S(2)}) copy-start(s32[4]{0:T(128)} %copy-done.21) | copy-start | bytes 52
  101.2 18.6 %copy-start.23 = (s32[4]{0:T(128)S(1)}, s32[4]{0:T(128)}, u32[]{:S(2)}) copy-start(s32[4]{0:T(128)} %get-tuple-element.40) | copy-start | bytes 52
  114.1 21.8 %collective-permute-start.14 = (bf16[208,640]{1,0:T(8,128)(2,1)}, bf16[208,640]{1,0:T(8,128)(2,1)S(1)}, u32[]{:S(2)}, u32[]{:S(2)}) collective-permute-start(bf16[208,640]{1,0:T(8,128)(2,1)} %get-tuple-element.25), channel_id=1, source_target_pairs={{0,48},{16,0},{32,16},{48,32},{1,49},{17,1},{33,17},{49,33},{2,50}... | collective-permute-start | bytes 798728 | tf_op jit(solution)/shard_map/ppermute | solution.py:36
  114.1 22.2 %collective-permute-start.15 = (bf16[208,640]{1,0:T(8,128)(2,1)}, bf16[208,640]{1,0:T(8,128)(2,1)S(1)}, u32[]{:S(2)}, u32[]{:S(2)}) collective-permute-start(bf16[208,640]{1,0:T(8,128)(2,1)} %get-tuple-element.26), channel_id=1, source_target_pairs={{0,16},{16,32},{32,48},{48,0},{1,17},{17,33},{33,49},{49,1},{2,18}... | collective-permute-start | bytes 798728 | tf_op jit(solution)/shard_map/ppermute | solution.py:36
  116.1 22.2 %collective-permute-start.16 = (bf16[208,640]{1,0:T(8,128)(2,1)}, bf16[208,640]{1,0:T(8,128)(2,1)S(1)}, u32[]{:S(2)}, u32[]{:S(2)}) collective-permute-start(bf16[208,640]{1,0:T(8,128)(2,1)} %get-tuple-element.27), channel_id=1, source_target_pairs={{0,32},{16,48},{32,0},{48,16},{1,33},{17,49},{33,1},{49,17},{2,34}... | collective-permute-start | bytes 798728 | tf_op jit(solution)/shard_map/ppermute | solution.py:36
  135.9 2.5 %copy-start.15 = (bf16[208,640]{1,0:T(8,128)(2,1)}, bf16[208,640]{1,0:T(8,128)(2,1)S(1)}, u32[]{:S(2)}) copy-start(bf16[208,640]{1,0:T(8,128)(2,1)S(1)} %collective-permute-done.14.a1) | copy-start | bytes 798724
  135.9 14.1 %collective-permute-start.17 = (bf16[208,640]{1,0:T(8,128)(2,1)}, bf16[208,640]{1,0:T(8,128)(2,1)}, u32[]{:S(2)}, u32[]{:S(2)}) collective-permute-start(bf16[208,640]{1,0:T(8,128)(2,1)} %get-tuple-element.29), channel_id=1, source_target_pairs={{0,72},{64,0},{8,64},{72,8},{1,73},{65,1},{9,65},{73,9},{2,74},{66... | collective-permute-start | bytes 798728 | tf_op jit(solution)/shard_map/ppermute | solution.py:40
  136.3 2.1 %copy-start.16 = (bf16[208,640]{1,0:T(8,128)(2,1)}, bf16[208,640]{1,0:T(8,128)(2,1)S(1)}, u32[]{:S(2)}) copy-start(bf16[208,640]{1,0:T(8,128)(2,1)S(1)} %collective-permute-done.15.a2) | copy-start | bytes 798724
  136.3 13.8 %collective-permute-start.18 = (bf16[208,640]{1,0:T(8,128)(2,1)}, bf16[208,640]{1,0:T(8,128)(2,1)}, u32[]{:S(2)}, u32[]{:S(2)}) collective-permute-start(bf16[208,640]{1,0:T(8,128)(2,1)} %get-tuple-element.31), channel_id=1, source_target_pairs={{0,64},{64,8},{8,72},{72,0},{1,65},{65,9},{9,73},{73,1},{2,66},{66... | collective-permute-start | bytes 798728 | tf_op jit(solution)/shard_map/ppermute | solution.py:40
  138.3 0.7 copy-start.17
  138.3 11.8 %collective-permute-start.19 = (bf16[208,640]{1,0:T(8,128)(2,1)}, bf16[208,640]{1,0:T(8,128)(2,1)}, u32[]{:S(2)}, u32[]{:S(2)}) collective-permute-start(bf16[208,640]{1,0:T(8,128)(2,1)} %get-tuple-element.32), channel_id=1, source_target_pairs={{0,8},{64,72},{8,0},{72,64},{1,9},{65,73},{9,1},{73,65},{2,10},{66... | collective-permute-start | bytes 798728 | tf_op jit(solution)/shard_map/ppermute | solution.py:40
  138.3 25.3 %collective-permute-start.24 = (bf16[384,3072]{1,0:T(8,128)(2,1)}, bf16[384,3072]{1,0:T(8,128)(2,1)}, u32[]{:S(2)}, u32[]{:S(2)}) collective-permute-start(bf16[384,3072]{1,0:T(8,128)(2,1)} %collective-permute-done.23.refs_2_), channel_id=1, source_target_pairs={{0,1},{1,0},{2,3},{3,2},{4,5},{5,4},{6,7},{7,6},{8,9},{9,8},{10,11... | collective-permute-start | bytes 7077896 | tf_op jit(solution)/shard_map/ppermute | solution.py:44
  139.0 24.6 %collective-permute-start.26 = (bf16[384,3072]{1,0:T(8,128)(2,1)}, bf16[384,3072]{1,0:T(8,128)(2,1)S(1)}, u32[]{:S(2)}, u32[]{:S(2)}) collective-permute-start(bf16[384,3072]{1,0:T(8,128)(2,1)} %collective-permute-done.25.refs_4_), channel_id=1, source_target_pairs={{0,1},{1,0},{2,3},{3,2},{4,5},{5,4},{6,7},{7,6},{8,9},{9,8},{10,11... | collective-permute-start | bytes 7077896 | tf_op jit(solution)/shard_map/ppermute | solution.py:44
  153.4 1.9 %collective-permute-start.20 = (bf16[320,384]{1,0:T(8,128)(2,1)}, bf16[320,384]{1,0:T(8,128)(2,1)S(1)}, u32[]{:S(2)}, u32[]{:S(2)}) collective-permute-start(bf16[320,384]{1,0:T(8,128)(2,1)} %get-tuple-element.34), channel_id=1, source_target_pairs={{0,1},{1,0},{2,3},{3,2},{4,5},{5,4},{6,7},{7,6},{8,9},{9,8},{10,11... | collective-permute-start | bytes 737288 | tf_op jit(solution)/shard_map/ppermute | solution.py:44
  155.3 3.4 %copy-start.7 = (bf16[320,384]{1,0:T(8,128)(2,1)}, bf16[320,384]{1,0:T(8,128)(2,1)S(1)}, u32[]{:S(2)}) copy-start(bf16[320,384]{1,0:T(8,128)(2,1)S(1)} %collective-permute-done.20.theirs) | copy-start | bytes 737284
  155.3 8.2 %collective-permute-start.21 = (bf16[160,384]{1,0:T(8,128)(2,1)S(1)}, bf16[160,384]{1,0:T(8,128)(2,1)S(1)}, u32[]{:S(2)}, u32[]{:S(2)}) collective-permute-start(bf16[160,384]{1,0:T(8,128)(2,1)S(1)} %pad_maximum_fusion.1), channel_id=1, source_target_pairs={{0,2},{2,4},{4,6},{6,0},{1,3},{3,5},{5,7},{7,1},{8,10},{10,12},{12... | collective-permute-start | bytes 368648 | tf_op jit(solution)/shard_map/ppermute | solution.py:32
  155.4 8.1 %collective-permute-start.22 = (bf16[160,384]{1,0:T(8,128)(2,1)S(1)}, bf16[160,384]{1,0:T(8,128)(2,1)S(1)}, u32[]{:S(2)}, u32[]{:S(2)}) collective-permute-start(bf16[160,384]{1,0:T(8,128)(2,1)S(1)} %pad_maximum_fusion.2), channel_id=1, source_target_pairs={{0,6},{2,0},{4,2},{6,4},{1,7},{3,1},{5,3},{7,5},{8,14},{10,8},{12,... | collective-permute-start | bytes 368648 | tf_op jit(solution)/shard_map/ppermute | solution.py:32
  163.5 14.6 %collective-permute-start.27 = (bf16[80,3072]{1,0:T(8,128)(2,1)}, bf16[80,3072]{1,0:T(8,128)(2,1)S(1)}, u32[]{:S(2)}, u32[]{:S(2)}) collective-permute-start(bf16[80,3072]{1,0:T(8,128)(2,1)} %far_output.1), channel_id=1, source_target_pairs={{0,4},{2,6},{4,0},{6,2},{1,5},{3,7},{5,1},{7,3},{8,12},{10,14},{12... | collective-permute-start | bytes 1474568 | tf_op jit(solution)/shard_map/ppermute | solution.py:32
  163.5 0.7 copy-start.18
  163.6 0.7 copy-start.19
  164.3 1.4 copy-start.6
